TPU v7x, 512 devices: a whole 4x8x8 slice. The times are simulated.
512 devices in a mesh: row: 16 (over z, core), col: 32 (over x, y).
Axes of the slice: x: 4, y: 8, z: 8, core: 2. Of those that a mesh axis runs over, the one named last changes fastest.
Arguments:
- state_fields: bfloat16 [4, 16, 16, 16, 32, 256], P(None, None, None, 'row', 'col'), may hold values from -6 to 6
- leaf_solve: float32 [256, 256], replicated, may hold values from -0.375 to 0.375
- leaf_flux: float32 [64, 256], replicated, may hold values from -0.375 to 0.375
- lift_edges: float32 [64, 128], replicated, may hold values from -4 to 4
- lift_leaves: float32 [256, 128], replicated, may hold values from -0.046875 to 0.046875
- merge_interface: float32 [5, 128, 128], replicated, may hold values from -0.25 to 0.25
- merge_parent: float32 [5, 256, 128], replicated, may hold values from -0.375 to 0.375
- split_child: float32 [5, 128, 256], replicated, may hold values from -0.5 to 0.5
- top_inverse: float32 [2048, 2048], P(None, 'row'), may hold values from -0.125 to 0.125
- spread_edges: float32 [64, 128], replicated, may hold values from -4 to 4
- spread_leaves: float32 [256, 128], replicated, may hold values from -0.5 to 0.5
- leaf_extend: float32 [256, 64], replicated, may hold values from -0.375 to 0.375
Outputs:
- new_fields: bfloat16 [4, 16, 16, 16, 32, 256], P(None, None, None, 'row', 'col')
All inputs are finite; a program needn't handle non-finite values.
Results may differ from a plain program's by a relative error of at most 0.0035.
Values may be sent and summed in bfloat16 or wider, within the bound.
A program may use at most 64 MiB of HBM per device.

v0:
```python
import jax
import jax.numpy as jnp
import numpy as np
from jax import lax
from jax.sharding import PartitionSpec as P

SKEL = 128
LR = 4
LC = 64


advect_scale = 0.01
full_precision = lax.Precision.HIGHEST


def extended(x, sides, width):
    for axis, dim in sides:
        devices, length = (lax.axis_size(axis), x.shape[dim])
        up = [(i, (i + 1) % devices) for i in range(devices)]
        down = [(j, i) for i, j in up]
        last = lax.slice_in_dim(x, length - width, length, axis=dim)
        first = lax.slice_in_dim(x, 0, width, axis=dim)
        before = lax.ppermute(last, axis, up)
        after = lax.ppermute(first, axis, down)
        x = jnp.concatenate([before, x, after], axis=dim)
    return x


def partner_2(block, axis, stride):
    count = lax.axis_size(axis)
    route = []
    for low in range(count):
        high = low | 1 << stride
        if high != low and high < count:
            route += [(low, high), (high, low)]
    return lax.ppermute(block, axis, route)


def chebyshev_matrix(node_count):
    points = np.arange(node_count)
    grid_x = np.cos(np.pi * points / (node_count - 1))
    weights = np.where(points == 0, 2.0, np.where(points == node_count - 1, 2.0, 1.0))
    parity = np.where((points[:, None] + points[None, :]) % 2 == 0, 1.0, -1.0)
    identity = np.eye(node_count)
    spacing = grid_x[:, None] - grid_x[None, :] + identity
    off_diagonal = weights[:, None] / weights[None, :] * parity / spacing * (1.0 - identity)
    result_matrix = off_diagonal - identity * off_diagonal.sum(axis=1)[:, None]
    return jnp.asarray(result_matrix, dtype=jnp.float32)


def tendency(values):
    derivative = chebyshev_matrix(values.shape[1])
    along_rows = jnp.einsum("ik,fkjrc->fijrc", derivative, values, precision=full_precision)
    along_cols = jnp.einsum("jk,fikrc->fijrc", derivative, values, precision=full_precision)
    return advect_scale * (values[0:1] * along_rows + values[1:2] * along_cols)


def average_rows(values, north_in, south_in):
    above = jnp.concatenate([north_in, values[:, -1, :, :-1, :]], axis=2)
    below = jnp.concatenate([values[:, 0, :, 1:, :], south_in], axis=2)
    first_row = (values[:, 0] + above) * 0.5
    last_row = (values[:, -1] + below) * 0.5
    return jnp.concatenate([first_row[:, None], values[:, 1:-1], last_row[:, None]], axis=1)


def average_cols(values, west_in, east_in):
    left_side = jnp.concatenate([west_in, values[:, :, -1, :, :-1]], axis=3)
    right_side = jnp.concatenate([values[:, :, 0, :, 1:], east_in], axis=3)
    first_col = (values[:, :, 0] + left_side) * 0.5
    last_col = (values[:, :, -1] + right_side) * 0.5
    return jnp.concatenate(
        [first_col[:, :, None], values[:, :, 1:-1], last_col[:, :, None]], axis=2
    )


def local(
    state_fields,
    leaf_solve,
    leaf_flux,
    lift_edges,
    lift_leaves,
    merge_interface,
    merge_parent,
    split_child,
    top_inverse,
    spread_edges,
    spread_leaves,
    leaf_extend,
):
    field_count = state_fields.shape[0]
    node_count = state_fields.shape[1]
    leaf_total = state_fields.shape[-1]
    local_grid = state_fields.reshape(field_count, node_count, node_count, LR, LC)
    widened = extended(local_grid, (("row", 3), ("col", 4)), 1)
    pushed = tendency(widened.astype(jnp.float32))
    rows_done = average_rows(pushed, pushed[:, -1][:, :, :1, :], pushed[:, 0][:, :, -1:, :])
    both_done = average_cols(
        rows_done, rows_done[:, :, -1][:, :, :, :1], rows_done[:, :, 0][:, :, :, -1:]
    )
    averaged = both_done[:, :, :, 1:-1, 1:-1]
    values = local_grid.astype(jnp.float32)
    source = (values - averaged).reshape(field_count, node_count * node_count, leaf_total)
    particular = jnp.einsum("nm,fml->fnl", leaf_solve, source, precision=full_precision)
    edge_flux = jnp.einsum("em,fml->fel", leaf_flux, source, precision=full_precision)
    lifted = jnp.einsum("fel,lb->feb", edge_flux, lift_leaves, precision=full_precision)
    skeleton = jnp.sum(lifted * lift_edges[None], axis=1)
    column = lax.axis_index("col")
    level_count = lax.axis_size("col").bit_length() - 1
    interfaces = []
    for merge_level in range(level_count):
        stride = 1 << merge_level
        partner = partner_2(skeleton, "col", merge_level)
        on_left = column // stride % 2 == 0
        left_half = jnp.where(on_left, skeleton, partner)
        right_half = jnp.where(on_left, partner, skeleton)
        interfaces.append(
            jnp.dot(right_half - left_half, merge_interface[merge_level], precision=full_precision)
        )
        joined = jnp.concatenate([left_half, right_half], axis=-1)
        skeleton = jnp.dot(joined, merge_parent[merge_level], precision=full_precision)
    shard_piece = lax.all_gather(skeleton[None], "row", axis=0, tiled=True)
    piece_rows = shard_piece.shape[0]
    top_rows = top_inverse
    top_rows = top_rows.reshape(piece_rows, SKEL, SKEL)
    boundary = jnp.einsum("gfb,gbc->fc", shard_piece, top_rows, precision=full_precision)
    for merge_level in reversed(range(level_count)):
        stride = 1 << merge_level
        child_map = split_child[merge_level]
        left_half = (
            jnp.dot(boundary, child_map[:, :SKEL], precision=full_precision)
            + interfaces[merge_level]
        )
        right_half = (
            jnp.dot(boundary, child_map[:, SKEL:], precision=full_precision)
            + interfaces[merge_level]
        )
        boundary = jnp.where(column // stride % 2 == 0, left_half, right_half)
    weighted = boundary[:, None, :] * spread_edges[None]
    spread = jnp.einsum("feb,lb->fel", weighted, spread_leaves, precision=full_precision)
    solved = particular + jnp.einsum("ne,fel->fnl", leaf_extend, spread, precision=full_precision)
    return solved.reshape(field_count, node_count, node_count, 1, 1, leaf_total).astype(
        jnp.bfloat16
    )


def solution(mesh):
    in_specs = (
        P(None, None, None, "row", "col", None),
        P(),
        P(),
        P(),
        P(),
        P(),
        P(),
        P(),
        P(None, "row"),
        P(),
        P(),
        P(),
    )
    out_specs = P(None, None, None, "row", "col", None)
    return jax.shard_map(local, mesh=mesh, in_specs=in_specs, out_specs=out_specs, check_vma=False)
```

profile of v0, /device:TPU:1, one launch (start us, length us, event | category | flops | bytes accessed | tf_op | source)
XLA Modules:
  0.0 127.9 jit_solution(2190358243321352747)
XLA Ops:
  0.0 2.1 %reshape.38 = bf16[4,16,16,4,64]{4,3,2,1,0:T(4,128)(2,1)S(1)} reshape(bf16[4,16,16,1,1,256]{5,2,4,3,1,0:T(8,128)(2,1)} %param.13) | data formatting | bytes 1048576 | tf_op jit(solution)/shard_map/reshape | solution.py:93
  2.1 0.7 fusion.100
  3.1 3.5 %collective-permute-start = (bf16[4,16,16,1,64]{4,1,3,2,0:T(8,128)(2,1)S(1)}, bf16[4,16,16,1,64]{4,1,3,2,0:T(8,128)(2,1)S(1)}, u32[]{:S(2)}, u32[]{:S(2)}) collective-permute-start(bf16[4,16,16,1,64]{4,1,3,2,0:T(8,128)(2,1)S(1)} %copy.84), channel_id=1, source_target_pairs={{0,32},{32,64},{64,96},{96,128},{128,160},{160,192},{192,224},{224... | collective-permute-start | bytes 393224 | tf_op jit(solution)/shard_map/ppermute | solution.py:23
  6.7 3.4 %collective-permute-start.1 = (bf16[4,16,16,1,64]{4,1,3,2,0:T(8,128)(2,1)S(1)}, bf16[4,16,16,1,64]{4,1,3,2,0:T(8,128)(2,1)S(1)}, u32[]{:S(2)}, u32[]{:S(2)}) collective-permute-start(bf16[4,16,16,1,64]{4,1,3,2,0:T(8,128)(2,1)S(1)} %copy.85), channel_id=1, source_target_pairs={{32,0},{64,32},{96,64},{128,96},{160,128},{192,160},{224,192},{256... | collective-permute-start | bytes 393224 | tf_op jit(solution)/shard_map/ppermute | solution.py:24
  10.1 0.8 collective-permute-done
  11.0 1.3 %constant_dynamic-update-slice_fusion.1 = bf16[4,16,16,6,64]{4,1,3,2,0:T(8,128)(2,1)S(1)} fusion(bf16[4,16,16,6,64]{4,1,3,2,0:T(8,128)(2,1)S(1)} %constant_dynamic-update-slice_fusion.2, bf16[4,16,16,4,64]{4,3,2,1,0:T(4,128)(2,1)S(1)} %reshape.38), kind=kLoop, calls=%fused_computation.110 | loop fusion | bytes 2097152
  12.2 0.3 collective-permute-done.1
  12.6 2.4 %fusion.99 = (bf16[4,16,16,6,1]{4,1,3,2,0:T(8,128)(2,1)}, bf16[4,16,16,6,1]{4,1,3,2,0:T(8,128)(2,1)}) fusion(bf16[4,16,16,6,64]{4,1,3,2,0:T(8,128)(2,1)S(1)} %constant_dynamic-update-slice_fusion), kind=kLoop, calls=%fused_computation.150 | loop fusion | bytes 49152 | tf_op jit(solution)/shard_map/slice | solution.py:21
  14.9 3.7 %copy.58 = bf16[4,16,16,6,1]{2,1,4,3,0:T(8,128)(2,1)S(1)} copy(bf16[4,16,16,6,1]{4,1,3,2,0:T(8,128)(2,1)} %get-tuple-element.19) | data formatting | bytes 24576 | tf_op jit(solution)/shard_map/slice | solution.py:21
  18.6 3.2 %collective-permute-start.2 = (bf16[4,16,16,6,1]{2,1,4,3,0:T(8,128)(2,1)S(1)}, bf16[4,16,16,6,1]{2,1,4,3,0:T(8,128)(2,1)}, u32[]{:S(2)}, u32[]{:S(2)}) collective-permute-start(bf16[4,16,16,6,1]{2,1,4,3,0:T(8,128)(2,1)S(1)} %copy.58), channel_id=1, source_target_pairs={{0,1},{1,2},{2,3},{3,4},{4,5},{5,6},{6,7},{7,8},{8,9},{9,10},{10,1... | collective-permute-start | bytes 36872 | tf_op jit(solution)/shard_map/ppermute | solution.py:23
  21.8 4.2 %copy.59 = bf16[4,16,16,6,1]{2,1,4,3,0:T(8,128)(2,1)} copy(bf16[4,16,16,6,1]{4,1,3,2,0:T(8,128)(2,1)} %get-tuple-element.20) | data formatting | bytes 24576 | tf_op jit(solution)/shard_map/slice | solution.py:22
  26.0 6.0 %collective-permute-start.3 = (bf16[4,16,16,6,1]{2,1,4,3,0:T(8,128)(2,1)}, bf16[4,16,16,6,1]{2,1,4,3,0:T(8,128)(2,1)}, u32[]{:S(2)}, u32[]{:S(2)}) collective-permute-start(bf16[4,16,16,6,1]{2,1,4,3,0:T(8,128)(2,1)} %copy.59), channel_id=1, source_target_pairs={{1,0},{2,1},{3,2},{4,3},{5,4},{6,5},{7,6},{8,7},{9,8},{10,9},{11,1... | collective-permute-start | bytes 36872 | tf_op jit(solution)/shard_map/ppermute | solution.py:24
  32.2 4.6 %copy.60 = bf16[4,16,16,6,1]{4,1,3,2,0:T(8,128)(2,1)} copy(bf16[4,16,16,6,1]{2,1,4,3,0:T(8,128)(2,1)} %collective-permute-done.2) | data formatting | bytes 24576 | tf_op jit(solution)/shard_map/ppermute | solution.py:23
  36.8 4.6 %copy.61 = bf16[4,16,16,6,1]{4,1,3,2,0:T(8,128)(2,1)} copy(bf16[4,16,16,6,1]{2,1,4,3,0:T(8,128)(2,1)} %collective-permute-done.3) | data formatting | bytes 24576 | tf_op jit(solution)/shard_map/ppermute | solution.py:24
  41.4 3.8 %fusion.96 = (f32[4,16,16,6,66]{4,1,3,2,0:T(8,128)S(1)}, bf16[4,16,16,6,66]{4,1,3,2,0:T(8,128)(2,1)S(1)}) fusion(bf16[4,16,16,6,1]{4,1,3,2,0:T(8,128)(2,1)} %copy.61, bf16[4,16,16,6,64]{4,1,3,2,0:T(8,128)(2,1)} %copy-done.2, bf16[4,16,16,6,1]{4,1,3,2,0:T(8,128)(2,1)} %copy.60), kind=kLoop, calls=%fused_computation.147 | loop fusion | flops 2838528 | bytes 3244032 | tf_op jit(solution)/shard_map/convert_element_type | solution.py:95
  45.3 0.6 copy-done.14
  45.9 1.5 %fusion.3 = f32[4,16,6,66,16]{3,4,2,1,0:T(8,128)S(1)} fusion(f32[16,16,1,1,1]{1,0,4,3,2:T(8,128)S(1)} %copy-done.14, bf16[4,16,16,6,66]{4,1,3,2,0:T(8,128)(2,1)S(1)} %get-tuple-element.6), kind=kOutput, calls=%fused_computation.9 | convolution fusion | flops 77856768 | bytes 2434048 | tf_op jit(solution)/shard_map/jk,fikrc->fijrc/dot_general | solution.py:54
  47.4 3.5 %fusion.1 = f32[4,16,16,6,66]{4,1,3,2,0:T(8,128)S(1)} fusion(f32[4,16,6,66,16]{3,4,2,1,0:T(8,128)S(1)} %fusion.3, bf16[4,16,16,6,66]{4,1,3,2,0:T(8,128)(2,1)S(1)} %get-tuple-element.6, f32[16,16,1,1,1]{1,0,4,3,2:T(8,128)S(1)} %copy-done.14, f32[16,16,6,66]{3,0,2,1:T(8,128)S(1)} %get-tuple-element.18, f32[16,16,6,66]{3,0,2,1:T(8,128)S(1)} %get-tuple-element.17), kind=kOutput, calls=%fused_computation.3 | convolution fusion | flops 79478784 | bytes 4867072 | tf_op jit(solution)/shard_map/ik,fkjrc->fijrc/dot_general | solution.py:53
  50.9 0.3 fusion.97
  51.2 0.2 fusion.98
  51.4 0.4 slice.198
  51.8 0.7 fusion.22
  52.5 0.8 pad_maximum_fusion
  53.5 1.6 %copy-done.3 = f32[4,16,16,6,66]{4,1,3,2,0:T(8,128)} copy-done((f32[4,16,16,6,66]{4,1,3,2,0:T(8,128)}, f32[4,16,16,6,66]{4,1,3,2,0:T(8,128)S(1)}, u32[]{:S(2)}) %copy-start.3) | copy-done | bytes 1622040
  55.4 0.2 copy.71
  55.9 0.2 copy.69
  56.1 1.7 %fusion.19 = (f32[4,16,1,6,66]{4,1,3,2,0:T(8,128)S(1)}, f32[4,16,1,6,66]{4,1,3,2,0:T(8,128)S(1)}) fusion(f32[4,1,16,6,66]{4,1,3,2,0:T(1,128)S(1)} %get-tuple-element.12, f32[4,14,16,6,66]{4,1,3,2,0:T(8,128)} %copy-done.1, f32[4,1,16,6,66]{4,1,3,2,0:T(1,128)S(1)} %get-tuple-element.11, f32[4,16,1,6,1]{4,1,3,2,0:T(8,128)S(1)} %copy.69, ...), kind=kLoop, calls=%fused_computation.45 | loop fusion | flops 354816 | bytes 1827840 | tf_op jit(solution)/shard_map/mul | solution.py:69
  57.8 0.4 slice-done
  58.2 1.5 %fusion.2 = f32[4,16,16,4,64]{4,1,3,2,0:T(8,128)S(1)} fusion(f32[4,16,1,6,66]{4,1,3,2,0:T(8,128)S(1)} %get-tuple-element.8, f32[4,16,14,6,66]{4,1,3,2,0:T(8,128)S(1)} %slice-done, f32[4,16,1,6,66]{4,1,3,2,0:T(8,128)S(1)} %get-tuple-element.7, bf16[4,16,16,4,64]{4,3,2,1,0:T(4,128)(2,1)S(1)} %reshape.38), kind=kLoop, calls=%fused_computation.6 | loop fusion | flops 1048576 | bytes 3194880 | tf_op jit(solution)/shard_map/sub | solution.py:102
  59.7 2.4 %copy.72 = f32[4,16,16,4,64]{4,3,2,1,0:T(4,128)} copy(f32[4,16,16,4,64]{4,1,3,2,0:T(8,128)S(1)} %fusion.2) | data formatting | bytes 2097152 | tf_op jit(solution)/shard_map/sub | solution.py:102
  62.1 2.5 %reshape.39 = f32[4,256,256]{2,1,0:T(8,128)S(1)} reshape(f32[4,16,16,4,64]{4,3,2,1,0:T(4,128)} %copy.72) | data formatting | bytes 2097152 | tf_op jit(solution)/shard_map/reshape | solution.py:102
  64.7 0.8 convolution_bitcast_fusion
  65.5 0.4 fusion.6
  65.9 2.1 %collective-permute-start.4 = (f32[4,128]{1,0:T(4,128)S(1)}, f32[4,128]{1,0:T(4,128)S(1)}, u32[]{:S(2)}, u32[]{:S(2)}) collective-permute-start(f32[4,128]{1,0:T(4,128)S(1)} %fusion.6), channel_id=1, source_target_pairs={{0,1},{1,0},{2,3},{3,2},{4,5},{5,4},{6,7},{7,6},{8,9},{9,8},{10,11... | collective-permute-start | bytes 6152 | tf_op jit(solution)/shard_map/ppermute | solution.py:36
  68.0 1.1 fusion.12
  69.1 1.3 %collective-permute-done.4 = f32[4,128]{1,0:T(4,128)S(1)} collective-permute-done((f32[4,128]{1,0:T(4,128)S(1)}, f32[4,128]{1,0:T(4,128)S(1)}, u32[]{:S(2)}, u32[]{:S(2)}) %collective-permute-start.4) | collective-permute-done | bytes 2080 | tf_op jit(solution)/shard_map/ppermute | solution.py:36
  70.6 1.9 %collective-permute-start.5 = (f32[4,128]{1,0:T(4,128)S(1)}, f32[4,128]{1,0:T(4,128)S(1)}, u32[]{:S(2)}, u32[]{:S(2)}) collective-permute-start(f32[4,128]{1,0:T(4,128)S(1)} %fusion.33), channel_id=1, source_target_pairs={{0,2},{2,0},{1,3},{3,1},{4,6},{6,4},{5,7},{7,5},{8,10},{10,8},{9,1... | collective-permute-start | bytes 6152 | tf_op jit(solution)/shard_map/ppermute | solution.py:36
  72.7 3.1 %collective-permute-done.5 = f32[4,128]{1,0:T(4,128)S(1)} collective-permute-done((f32[4,128]{1,0:T(4,128)S(1)}, f32[4,128]{1,0:T(4,128)S(1)}, u32[]{:S(2)}, u32[]{:S(2)}) %collective-permute-start.5) | collective-permute-done | bytes 2080 | tf_op jit(solution)/shard_map/ppermute | solution.py:36
  76.0 4.7 %collective-permute-start.6 = (f32[4,128]{1,0:T(4,128)S(1)}, f32[4,128]{1,0:T(4,128)S(1)}, u32[]{:S(2)}, u32[]{:S(2)}) collective-permute-start(f32[4,128]{1,0:T(4,128)S(1)} %fusion.31), channel_id=1, source_target_pairs={{0,4},{4,0},{1,5},{5,1},{2,6},{6,2},{3,7},{7,3},{8,12},{12,8},{9,1... | collective-permute-start | bytes 6152 | tf_op jit(solution)/shard_map/ppermute | solution.py:36
  80.9 3.3 %collective-permute-done.6 = f32[4,128]{1,0:T(4,128)S(1)} collective-permute-done((f32[4,128]{1,0:T(4,128)S(1)}, f32[4,128]{1,0:T(4,128)S(1)}, u32[]{:S(2)}, u32[]{:S(2)}) %collective-permute-start.6) | collective-permute-done | bytes 2080 | tf_op jit(solution)/shard_map/ppermute | solution.py:36
  84.4 1.9 %collective-permute-start.7 = (f32[4,128]{1,0:T(4,128)S(1)}, f32[4,128]{1,0:T(4,128)S(1)}, u32[]{:S(2)}, u32[]{:S(2)}) collective-permute-start(f32[4,128]{1,0:T(4,128)S(1)} %fusion.29), channel_id=1, source_target_pairs={{0,8},{8,0},{1,9},{9,1},{2,10},{10,2},{3,11},{11,3},{4,12},{12,4},... | collective-permute-start | bytes 6152 | tf_op jit(solution)/shard_map/ppermute | solution.py:36
  86.5 2.2 %collective-permute-done.7 = f32[4,128]{1,0:T(4,128)S(1)} collective-permute-done((f32[4,128]{1,0:T(4,128)S(1)}, f32[4,128]{1,0:T(4,128)S(1)}, u32[]{:S(2)}, u32[]{:S(2)}) %collective-permute-start.7) | collective-permute-done | bytes 2080 | tf_op jit(solution)/shard_map/ppermute | solution.py:36
  88.9 2.8 %collective-permute-start.8 = (f32[4,128]{1,0:T(4,128)S(1)}, f32[4,128]{1,0:T(4,128)S(1)}, u32[]{:S(2)}, u32[]{:S(2)}) collective-permute-start(f32[4,128]{1,0:T(4,128)S(1)} %fusion.27), channel_id=1, source_target_pairs={{0,16},{16,0},{1,17},{17,1},{2,18},{18,2},{3,19},{19,3},{4,20},{20... | collective-permute-start | bytes 6152 | tf_op jit(solution)/shard_map/ppermute | solution.py:36
  91.9 2.8 %collective-permute-done.8 = f32[4,128]{1,0:T(4,128)S(1)} collective-permute-done((f32[4,128]{1,0:T(4,128)S(1)}, f32[4,128]{1,0:T(4,128)S(1)}, u32[]{:S(2)}, u32[]{:S(2)}) %collective-permute-start.8) | collective-permute-done | bytes 2080 | tf_op jit(solution)/shard_map/ppermute | solution.py:36
  95.1 28.3 %all-gather.1 = f32[16,4,128]{2,1,0:T(4,128)S(1)} all-gather(f32[1,4,128]{2,1,0:T(4,128)S(1)} %convolution_bitcast_fusion.2), channel_id=2, replica_groups=mesh['row'=16,'col'=32] {'row'}, dimensions={0}, use_global_device_ids=true | all-gather | bytes 34816 | tf_op jit(solution)/shard_map/all_gather | solution.py:121
  123.3 0.6 convolution_bitcast_fusion.1
  125.7 0.4 fusion.24
  126.1 1.8 %fusion.5 = bf16[4,256,256]{1,2,0:T(8,128)(2,1)} fusion(f32[4,256,256]{1,2,0:T(8,128)S(1)} %fusion.12, f32[4,64,256]{2,1,0:T(8,128)S(1)} %fusion.24, f32[256,64]{0,1:T(8,128)S(1)} %copy-done.11), kind=kOutput, calls=%fused_computation.12 | convolution fusion | flops 201850880 | bytes 1900544 | tf_op jit(solution)/shard_map/ne,fel->fnl/dot_general | solution.py:140
  (69 shorter events, 4.7 us)
Async XLA Ops:
  0.0 123.3 %copy-start = (f32[2048,128]{1,0:T(8,128)S(1)}, f32[2048,128]{1,0:T(8,128)}, u32[]{:S(2)}) copy-start(f32[2048,128]{1,0:T(8,128)} %param.21) | copy-start | bytes 3145732
  3.1 7.9 %collective-permute-start = (bf16[4,16,16,1,64]{4,1,3,2,0:T(8,128)(2,1)S(1)}, bf16[4,16,16,1,64]{4,1,3,2,0:T(8,128)(2,1)S(1)}, u32[]{:S(2)}, u32[]{:S(2)}) collective-permute-start(bf16[4,16,16,1,64]{4,1,3,2,0:T(8,128)(2,1)S(1)} %copy.84), channel_id=1, source_target_pairs={{0,32},{32,64},{64,96},{96,128},{128,160},{160,192},{192,224},{224... | collective-permute-start | bytes 393224 | tf_op jit(solution)/shard_map/ppermute | solution.py:23
  6.7 5.8 %collective-permute-start.1 = (bf16[4,16,16,1,64]{4,1,3,2,0:T(8,128)(2,1)S(1)}, bf16[4,16,16,1,64]{4,1,3,2,0:T(8,128)(2,1)S(1)}, u32[]{:S(2)}, u32[]{:S(2)}) collective-permute-start(bf16[4,16,16,1,64]{4,1,3,2,0:T(8,128)(2,1)S(1)} %copy.85), channel_id=1, source_target_pairs={{32,0},{64,32},{96,64},{128,96},{160,128},{192,160},{224,192},{256... | collective-permute-start | bytes 393224 | tf_op jit(solution)/shard_map/ppermute | solution.py:24
  12.6 2.4 %copy-start.2 = (bf16[4,16,16,6,64]{4,1,3,2,0:T(8,128)(2,1)}, bf16[4,16,16,6,64]{4,1,3,2,0:T(8,128)(2,1)S(1)}, u32[]{:S(2)}) copy-start(bf16[4,16,16,6,64]{4,1,3,2,0:T(8,128)(2,1)S(1)} %constant_dynamic-update-slice_fusion) | copy-start | bytes 2359300
  14.9 17.1 %copy-start.4 = (f32[5,128,256]{2,1,0:T(8,128)S(1)}, f32[5,128,256]{2,1,0:T(8,128)}, u32[]{:S(2)}) copy-start(f32[5,128,256]{2,1,0:T(8,128)} %param.20) | copy-start | bytes 1966084
  18.6 13.6 %collective-permute-start.2 = (bf16[4,16,16,6,1]{2,1,4,3,0:T(8,128)(2,1)S(1)}, bf16[4,16,16,6,1]{2,1,4,3,0:T(8,128)(2,1)}, u32[]{:S(2)}, u32[]{:S(2)}) collective-permute-start(bf16[4,16,16,6,1]{2,1,4,3,0:T(8,128)(2,1)S(1)} %copy.58), channel_id=1, source_target_pairs={{0,1},{1,2},{2,3},{3,4},{4,5},{5,6},{6,7},{7,8},{8,9},{9,10},{10,1... | collective-permute-start | bytes 36872 | tf_op jit(solution)/shard_map/ppermute | solution.py:23
  26.0 10.8 %collective-permute-start.3 = (bf16[4,16,16,6,1]{2,1,4,3,0:T(8,128)(2,1)}, bf16[4,16,16,6,1]{2,1,4,3,0:T(8,128)(2,1)}, u32[]{:S(2)}, u32[]{:S(2)}) collective-permute-start(bf16[4,16,16,6,1]{2,1,4,3,0:T(8,128)(2,1)} %copy.59), channel_id=1, source_target_pairs={{1,0},{2,1},{3,2},{4,3},{5,4},{6,5},{7,6},{8,7},{9,8},{10,9},{11,1... | collective-permute-start | bytes 36872 | tf_op jit(solution)/shard_map/ppermute | solution.py:24
  45.2 0.7 copy-start.14
  51.8 1.6 %copy-start.1 = (f32[4,14,16,6,66]{4,1,3,2,0:T(8,128)}, f32[4,14,16,6,66]{4,1,3,2,0:T(8,128)S(1)}, u32[]{:S(2)}) copy-start(f32[4,14,16,6,66]{4,1,3,2,0:T(8,128)S(1)} %slice.198) | copy-start | bytes 4257796
  53.4 1.7 %copy-start.3 = (f32[4,16,16,6,66]{4,1,3,2,0:T(8,128)}, f32[4,16,16,6,66]{4,1,3,2,0:T(8,128)S(1)}, u32[]{:S(2)}) copy-start(f32[4,16,16,6,66]{4,1,3,2,0:T(8,128)S(1)} %pad_maximum_fusion) | copy-start | bytes 4866052
  56.1 2.1 %slice-start = ((f32[4,16,16,6,66]{4,1,3,2,0:T(8,128)}), f32[4,16,14,6,66]{4,1,3,2,0:T(8,128)S(1)}, s32[]{:S(2)}) async-start(f32[4,16,16,6,66]{4,1,3,2,0:T(8,128)} %copy-done.3), calls=%async_computation | async-start | bytes 5505024 | tf_op jit(solution)/shard_map/slice | solution.py:72
  62.1 2.6 %copy-start.10 = (f32[64,256]{1,0:T(8,128)S(1)}, f32[64,256]{1,0:T(8,128)}, u32[]{:S(2)}) copy-start(f32[64,256]{1,0:T(8,128)} %param.15) | copy-start | bytes 196612
  62.1 3.4 %copy-start.8 = (f32[256,128]{1,0:T(8,128)S(1)}, f32[256,128]{1,0:T(8,128)}, u32[]{:S(2)}) copy-start(f32[256,128]{1,0:T(8,128)} %param.17) | copy-start | bytes 393220
  62.1 3.4 %copy-start.12 = (f32[64,128]{1,0:T(8,128)S(1)}, f32[64,128]{1,0:T(8,128)}, u32[]{:S(2)}) copy-start(f32[64,128]{1,0:T(8,128)} %param.16) | copy-start | bytes 98308
  62.1 5.9 %copy-start.7 = (f32[256,256]{1,0:T(8,128)S(1)}, f32[256,256]{1,0:T(8,128)}, u32[]{:S(2)}) copy-start(f32[256,256]{1,0:T(8,128)} %param.14) | copy-start | bytes 786436
  64.7 5.7 %copy-start.5 = (f32[5,256,128]{2,1,0:T(8,128)S(1)}, f32[5,256,128]{2,1,0:T(8,128)}, u32[]{:S(2)}) copy-start(f32[5,256,128]{2,1,0:T(8,128)} %param.19) | copy-start | bytes 1966084
  64.7 7.8 %copy-start.6 = (f32[5,128,128]{2,1,0:T(8,128)S(1)}, f32[5,128,128]{2,1,0:T(8,128)}, u32[]{:S(2)}) copy-start(f32[5,128,128]{2,1,0:T(8,128)} %param.18) | copy-start | bytes 983044
  65.9 59.7 %copy-start.9 = (f32[256,128]{1,0:T(8,128)S(1)}, f32[256,128]{1,0:T(8,128)}, u32[]{:S(2)}) copy-start(f32[256,128]{1,0:T(8,128)} %param.23) | copy-start | bytes 393220
  65.9 59.8 %copy-start.13 = (f32[64,128]{1,0:T(8,128)S(1)}, f32[64,128]{1,0:T(8,128)}, u32[]{:S(2)}) copy-start(f32[64,128]{1,0:T(8,128)} %param.22) | copy-start | bytes 98308
  65.9 4.5 %collective-permute-start.4 = (f32[4,128]{1,0:T(4,128)S(1)}, f32[4,128]{1,0:T(4,128)S(1)}, u32[]{:S(2)}, u32[]{:S(2)}) collective-permute-start(f32[4,128]{1,0:T(4,128)S(1)} %fusion.6), channel_id=1, source_target_pairs={{0,1},{1,0},{2,3},{3,2},{4,5},{5,4},{6,7},{7,6},{8,9},{9,8},{10,11... | collective-permute-start | bytes 6152 | tf_op jit(solution)/shard_map/ppermute | solution.py:36
  69.1 57.0 %copy-start.11 = (f32[256,64]{0,1:T(8,128)S(1)}, f32[256,64]{0,1:T(8,128)}, u32[]{:S(2)}) copy-start(f32[256,64]{0,1:T(8,128)} %param.24) | copy-start | bytes 196612
  70.6 5.2 %collective-permute-start.5 = (f32[4,128]{1,0:T(4,128)S(1)}, f32[4,128]{1,0:T(4,128)S(1)}, u32[]{:S(2)}, u32[]{:S(2)}) collective-permute-start(f32[4,128]{1,0:T(4,128)S(1)} %fusion.33), channel_id=1, source_target_pairs={{0,2},{2,0},{1,3},{3,1},{4,6},{6,4},{5,7},{7,5},{8,10},{10,8},{9,1... | collective-permute-start | bytes 6152 | tf_op jit(solution)/shard_map/ppermute | solution.py:36
  76.0 8.2 %collective-permute-start.6 = (f32[4,128]{1,0:T(4,128)S(1)}, f32[4,128]{1,0:T(4,128)S(1)}, u32[]{:S(2)}, u32[]{:S(2)}) collective-permute-start(f32[4,128]{1,0:T(4,128)S(1)} %fusion.31), channel_id=1, source_target_pairs={{0,4},{4,0},{1,5},{5,1},{2,6},{6,2},{3,7},{7,3},{8,12},{12,8},{9,1... | collective-permute-start | bytes 6152 | tf_op jit(solution)/shard_map/ppermute | solution.py:36
  84.4 4.3 %collective-permute-start.7 = (f32[4,128]{1,0:T(4,128)S(1)}, f32[4,128]{1,0:T(4,128)S(1)}, u32[]{:S(2)}, u32[]{:S(2)}) collective-permute-start(f32[4,128]{1,0:T(4,128)S(1)} %fusion.29), channel_id=1, source_target_pairs={{0,8},{8,0},{1,9},{9,1},{2,10},{10,2},{3,11},{11,3},{4,12},{12,4},... | collective-permute-start | bytes 6152 | tf_op jit(solution)/shard_map/ppermute | solution.py:36
  88.9 5.8 %collective-permute-start.8 = (f32[4,128]{1,0:T(4,128)S(1)}, f32[4,128]{1,0:T(4,128)S(1)}, u32[]{:S(2)}, u32[]{:S(2)}) collective-permute-start(f32[4,128]{1,0:T(4,128)S(1)} %fusion.27), channel_id=1, source_target_pairs={{0,16},{16,0},{1,17},{17,1},{2,18},{18,2},{3,19},{19,3},{4,20},{20... | collective-permute-start | bytes 6152 | tf_op jit(solution)/shard_map/ppermute | solution.py:36
where the time goes:
time: 128 us
  local copies, waits for them, and re-layouts  33.6 us (26%)
  starting transfers between devices  29.6 us (23%)
  blocking collectives  28.3 us (22%)
  waiting for transfers between devices  13.9 us (11%)
  matrix products  13.4 us (10%)
  other arithmetic  8.61 us (7%)
    all_gather x1, blocking collectives, local(): shard_piece = lax.all_gather(skeleton[None], 'row', axis=0, tiled=True)  28.3 us
    ppermute x5, starting transfers between devices, partner_2(): return lax.ppermute(block, axis, route)  13.5 us
    ppermute x5, waiting for transfers between devices, partner_2(): return lax.ppermute(block, axis, route)  12.8 us
    ppermute x2, starting transfers between devices, extended(): after = lax.ppermute(first, axis, down)  9.4 us
    ppermute x2, starting transfers between devices, extended(): before = lax.ppermute(last, axis, up)  6.69 us
    slice x2, local copies, waits for them, and re-layouts, extended(): last = lax.slice_in_dim(x, length - width, length, axis=dim)  6.02 us
    slice x2, local copies, waits for them, and re-layouts, extended(): first = lax.slice_in_dim(x, 0, width, axis=dim)  4.95 us
    ppermute x1, local copies, waits for them, and re-layouts, extended(): before = lax.ppermute(last, axis, up)  4.6 us
  transfers between devices with their start and end apart: 9, of which 7 were waited for; matrix products, arithmetic and copies ran while one was open for 9% of the time, Pallas kernels for 0%

commit v1 on v0

v1 whole, which is shorter than its diff:
```python
import jax
import jax.numpy as jnp
import numpy as np
from jax import lax
from jax.experimental import pallas as pl
from jax.experimental.pallas import tpu as pltpu
from jax.sharding import PartitionSpec as P

F32 = jnp.float32
BF16 = jnp.bfloat16
MESH = pl.DeviceIdType.MESH
LEVELS = 5
N_ROW = 16
N_COL = 32
advect_scale = 0.01


def chebyshev_matrix(node_count):
    points = np.arange(node_count)
    grid_x = np.cos(np.pi * points / (node_count - 1))
    weights = np.where(points == 0, 2.0, np.where(points == node_count - 1, 2.0, 1.0))
    parity = np.where((points[:, None] + points[None, :]) % 2 == 0, 1.0, -1.0)
    identity = np.eye(node_count)
    spacing = grid_x[:, None] - grid_x[None, :] + identity
    off_diagonal = weights[:, None] / weights[None, :] * parity / spacing * (1.0 - identity)
    result_matrix = off_diagonal - identity * off_diagonal.sum(axis=1)[:, None]
    return result_matrix.astype(np.float32)


def derivative_parts():
    d = chebyshev_matrix(16)
    eye = np.eye(16, dtype=np.float32)
    both = np.concatenate([np.kron(d, eye), np.kron(eye, d)], axis=0) * np.float32(advect_scale)
    high = both.astype(jnp.bfloat16)
    low = (both - high.astype(np.float32)).astype(jnp.bfloat16)
    return high, low


def face_columns():
    e = np.zeros((256, 64), np.float32)
    for k in range(16):
        e[k, k] = 1.0
        e[240 + k, 16 + k] = 1.0
        e[16 * k, 32 + k] = 1.0
        e[16 * k + 15, 48 + k] = 1.0
    return e.astype(jnp.bfloat16)


def split(x):
    high = x.astype(BF16)
    return high, (x - high.astype(F32)).astype(BF16)


def mm(a, b, dims=((1,), (0,))):
    return lax.dot_general(a, b, (dims, ((), ())), preferred_element_type=F32)


def dot3(a, b, dims=((1,), (0,))):
    return mm(a[0], b[0], dims) + mm(a[0], b[1], dims) + mm(a[1], b[0], dims)


def bit_reversed(m):
    return sum(((m >> k) & 1) << (LEVELS - 1 - k) for k in range(LEVELS))


def kernel(
    q_ref, solve_ref, flux_ref, lift_e_ref, lift_l_ref, mi_ref, parent_ref, child_ref, top_ref,
    spr_e_ref, spr_l_ref, ext_t_ref, der_h_ref, der_l_ref, face_ref,
    out_ref,
    tend_ref, part_ref, k_ref, src1, dst1, src2, dst2, src3, dst3, src4, dst4,
    par_h, par_l, top_h, top_l,
    send1, recv1, send2, recv2, send3, recv3, send4, recv4,
):
    row = lax.axis_index("row")
    col = lax.axis_index("col")
    bits = [(col // (1 << k)) % 2 for k in range(LEVELS)]

    def other(m):
        return sum(
            (1 - bits[k] if (m >> k) & 1 else bits[k]) * (1 << k) for k in range(LEVELS)
        )

    def row_at(d):
        return (row + d) % N_ROW

    barrier = pltpu.get_barrier_semaphore()
    for m in range(1, N_COL):
        pl.semaphore_signal(barrier, inc=1, device_id=(row, other(m)), device_id_type=MESH)
    for d in range(1, N_ROW):
        pl.semaphore_signal(barrier, inc=1, device_id=(row_at(d), col), device_id_type=MESH)

    der_h, der_l = der_h_ref[...], der_l_ref[...]
    q0 = q_ref[0:256, :].astype(F32)
    q1 = q_ref[256:512, :].astype(F32)
    for f in range(4):
        q = q_ref[256 * f : 256 * f + 256, :]
        both = mm(der_h, q) + mm(der_l, q)
        tend_ref[256 * f : 256 * f + 256, :] = q0 * both[:256] + q1 * both[256:]

    lane = lax.broadcasted_iota(jnp.int32, (64, 256), 1)
    half_lane = lax.broadcasted_iota(jnp.int32, (64, 128), 1)
    place = lax.broadcasted_iota(jnp.int32, (64, 256), 0) % 16

    def rows_of(first):
        return jnp.concatenate(
            [tend_ref[256 * f + first : 256 * f + first + 16, :] for f in range(4)], axis=0
        )

    def nodes_of(first):
        return tend_ref[...].reshape(64, 16, 256)[:, first, :]

    top, bottom = rows_of(0), rows_of(240)
    above = pltpu.roll(bottom, 64, 1)
    below = pltpu.roll(top, 192, 1)
    src1[0] = above[:, :128]
    src1[1] = below[:, 128:]
    pl.semaphore_wait(barrier, N_COL - 1 + N_ROW - 1)

    def remote(src, dst, send, recv, where):
        return pltpu.make_async_remote_copy(
            src_ref=src, dst_ref=dst, send_sem=send, recv_sem=recv, device_id=where,
            device_id_type=MESH,
        )

    south = remote(src1.at[0], dst1.at[0], send1.at[0], recv1.at[0], (row_at(1), col))
    north = remote(src1.at[1], dst1.at[1], send1.at[1], recv1.at[1], (row_at(N_ROW - 1), col))
    south.start()
    north.start()

    k_map = dot3(
        split(flux_ref[...].T), split(lift_e_ref[...])
    )
    k_ref[...] = k_map
    lift_l = split(lift_l_ref[...])
    own = []
    for f in range(4):
        q = q_ref[256 * f : 256 * f + 256, :].astype(F32)
        w = dot3(split(q - tend_ref[256 * f : 256 * f + 256, :]), lift_l)
        own.append(jnp.sum(w * k_map, axis=0, keepdims=True))
    left, right = nodes_of(0), nodes_of(15)

    south.wait()
    north.wait()
    above = jnp.where(lane < 64, jnp.concatenate([dst1[0], dst1[0]], axis=1), above)
    below = jnp.where(lane >= 192, jnp.concatenate([dst1[1], dst1[1]], axis=1), below)
    top_new = (top + above) * 0.5
    bottom_new = (bottom + below) * 0.5
    left_rows = jnp.where(
        place == 0, top_new, jnp.where(place == 15, pltpu.roll(bottom_new, 15, 0), left)
    )
    right_rows = jnp.where(
        place == 0, pltpu.roll(top_new, 49, 0), jnp.where(place == 15, bottom_new, right)
    )
    to_east = pltpu.roll(right_rows, 193, 1)
    to_west = pltpu.roll(left_rows, 63, 1)
    src2[0] = jnp.where(half_lane % 64 == 0, to_east[:, :128], pltpu.roll(to_east[:, 128:], 1, 1))
    src2[1] = jnp.where(half_lane % 64 == 63, to_west[:, :128], pltpu.roll(to_west[:, 128:], 1, 1))
    east = remote(src2.at[0], dst2.at[0], send2.at[0], recv2.at[0], (row, (col + 1) % N_COL))
    west = remote(
        src2.at[1], dst2.at[1], send2.at[1], recv2.at[1], (row, (col + N_COL - 1) % N_COL)
    )
    east.start()
    west.start()

    for k in range(LEVELS):
        whole = parent_ref[k]
        swapped = jnp.concatenate([whole[128:], whole[:128]], axis=0)
        high, low = split(jnp.where(bits[k] == 0, whole, swapped))
        par_h[k] = high
        par_l[k] = low

    east.wait()
    west.wait()

    def opened(received):
        return jnp.concatenate([received, pltpu.roll(received, 127, 1)], axis=1)

    before = jnp.where(lane % 64 == 0, opened(dst2[0]), pltpu.roll(right_rows, 1, 1))
    after = jnp.where(lane % 64 == 63, opened(dst2[1]), pltpu.roll(left_rows, 255, 1))
    inner = jnp.logical_and(place != 0, place != 15)
    deltas = [
        jnp.where(inner, top_new - top, 0.0),
        jnp.where(inner, bottom_new - bottom, 0.0),
        (left_rows + before) * 0.5 - left,
        (right_rows + after) * 0.5 - right,
    ]
    w = dot3(split(jnp.concatenate(deltas, axis=0)), lift_l)
    k_nodes = k_ref[...].reshape(16, 16, 128)
    k_faces = [k_nodes[0], k_nodes[15], k_nodes[:, 0, :], k_nodes[:, 15, :]]
    skeleton = []
    for f in range(4):
        change = sum(
            w[64 * s + 16 * f : 64 * s + 16 * f + 16] * k_faces[s] for s in range(4)
        )
        skeleton.append(own[f] - jnp.sum(change, axis=0, keepdims=True))
    skeleton = jnp.concatenate(skeleton, axis=0)
    src3[...] = skeleton
    dst3[0] = skeleton
    gathers = []
    for m in range(N_COL - 1, 0, -1):
        slot = bit_reversed(m)
        gathers.append(
            remote(src3, dst3.at[slot], send3.at[m], recv3.at[m], (row, other(m)))
        )
    for copy in gathers:
        copy.start()

    solve = split(solve_ref[...])
    face = face_ref[...]
    solve_face = (mm(solve[0], face).astype(BF16), mm(solve[1], face).astype(BF16))
    for f in range(4):
        q = q_ref[256 * f : 256 * f + 256, :].astype(F32)
        change = jnp.concatenate([d[16 * f : 16 * f + 16] for d in deltas], axis=0)
        part_ref[256 * f : 256 * f + 256, :] = dot3(
            solve, split(q - tend_ref[256 * f : 256 * f + 256, :])
        ) - dot3(solve_face, split(change))
    chain = None
    interface_maps = []
    for k in range(LEVELS):
        child = split(jnp.where(bits[k] == 0, child_ref[k, :, :128], child_ref[k, :, 128:]))
        sign = (1 - 2 * bits[k]).astype(F32)
        step = mi_ref[k] if chain is None else dot3(split(mi_ref[k]), chain)
        interface_maps.append(step * sign)
        chain = child if chain is None else split(dot3(child, chain))
    interface_map = split(jnp.concatenate(interface_maps, axis=0))
    for part in range(8):
        at = slice(256 * part, 256 * part + 256)
        high, low = split(dot3(split(top_ref[at, :]), chain))
        top_h[at, :] = high
        top_l[at, :] = low
    extend = dot3(split(ext_t_ref[...].T), split(spr_e_ref[...]))
    spread_l = split(spr_l_ref[...])

    for copy in gathers:
        copy.wait()
    x = dst3[...].reshape(4 * N_COL, 128)
    differences = []
    for k in range(LEVELS):
        rows = (4 * N_COL) >> (k + 1)
        first, second = x[:rows], x[rows:]
        differences.append((second - first)[:4])
        joined = jnp.concatenate([first, second], axis=1)
        x = dot3(split(joined), (par_h[k], par_l[k]))
    src4[...] = x
    dst4[row] = x
    sends = []
    arrivals = []
    for d in range(1, N_ROW):
        sends.append(remote(src4, dst4.at[row], send4.at[d], recv4.at[d], (row_at(d), col)))
        arrivals.append(
            remote(src4, dst4.at[row_at(N_ROW - d)], send4.at[d], recv4.at[d], (row_at(d), col))
        )
    for copy in sends:
        copy.start()
    boundary = dot3(split(jnp.concatenate(differences, axis=1)), interface_map)
    for copy in sends:
        copy.wait_send()
    for copy in arrivals:
        copy.wait_recv()
    pieces = split(jnp.concatenate([dst4[g] for g in range(N_ROW)], axis=1))
    boundary = boundary + dot3(pieces, (top_h[...], top_l[...]))
    for f in range(4):
        weighted = split(extend * boundary[f : f + 1, :])
        at = slice(256 * f, 256 * f + 256)
        out_ref[at, :] = (part_ref[at, :] + dot3(weighted, spread_l, ((1,), (1,)))).astype(BF16)


def local(
    state_fields, leaf_solve, leaf_flux, lift_edges, lift_leaves, merge_interface, merge_parent,
    split_child, top_inverse, spread_edges, spread_leaves, leaf_extend,
):
    der_h, der_l = derivative_parts()
    dma = pltpu.SemaphoreType.DMA
    result = pl.pallas_call(
        kernel,
        name="imex_step",
        out_shape=jax.ShapeDtypeStruct((1024, 256), BF16),
        in_specs=[pl.BlockSpec(memory_space=pltpu.VMEM)] * 15,
        out_specs=pl.BlockSpec(memory_space=pltpu.VMEM),
        scratch_shapes=[
            pltpu.VMEM((1024, 256), F32),
            pltpu.VMEM((1024, 256), F32),
            pltpu.VMEM((256, 128), F32),
            pltpu.VMEM((2, 64, 128), F32),
            pltpu.VMEM((2, 64, 128), F32),
            pltpu.VMEM((2, 64, 128), F32),
            pltpu.VMEM((2, 64, 128), F32),
            pltpu.VMEM((4, 128), F32),
            pltpu.VMEM((N_COL, 4, 128), F32),
            pltpu.VMEM((4, 128), F32),
            pltpu.VMEM((N_ROW, 4, 128), F32),
            pltpu.VMEM((LEVELS, 256, 128), BF16),
            pltpu.VMEM((LEVELS, 256, 128), BF16),
            pltpu.VMEM((2048, 128), BF16),
            pltpu.VMEM((2048, 128), BF16),
            dma((2,)), dma((2,)), dma((2,)), dma((2,)),
            dma((N_COL,)), dma((N_COL,)), dma((N_ROW,)), dma((N_ROW,)),
        ],
        compiler_params=pltpu.CompilerParams(
            collective_id=0, has_side_effects=True, vmem_limit_bytes=48 * 1024 * 1024
        ),
    )(
        state_fields.reshape(1024, 256), leaf_solve, leaf_flux, lift_edges, lift_leaves,
        merge_interface, merge_parent, split_child, top_inverse, spread_edges, spread_leaves,
        leaf_extend.T, jnp.asarray(der_h), jnp.asarray(der_l), jnp.asarray(face_columns()),
    )
    return result.reshape(state_fields.shape)


def solution(mesh):
    in_specs = (
        P(None, None, None, "row", "col", None),
        P(), P(), P(), P(), P(), P(), P(),
        P(None, "row"),
        P(), P(), P(),
    )
    out_specs = P(None, None, None, "row", "col", None)
    return jax.shard_map(local, mesh=mesh, in_specs=in_specs, out_specs=out_specs, check_vma=False)
```

time: 128 us -> 51.6 us (0.40)
  Pallas kernels: 0 us -> 36 us
  starting transfers between devices: 29.6 us -> 0 us
  blocking collectives: 28.3 us -> 0 us
  local copies, waits for them, and re-layouts: 33.6 us -> 14.9 us
  waiting for transfers between devices: 13.9 us -> 0 us
  matrix products: 13.4 us -> 0 us
  other arithmetic: 8.61 us -> 0 us
    pallas_call x0 -> x1, Pallas kernels: none -> 36 us  [local(): pl.pallas_call(kernel, name='imex_step', out_shape=jax.ShapeDtypeStruct((...]
    ppermute x9 -> x0, starting transfers between devices: 29.6 us -> none  [the longest x5 13.5 us: partner_2(): return lax.ppermute(block, axis, route)]
    all_gather x1 -> x0, blocking collectives: 28.3 us -> none  [local(): shard_piece = lax.all_gather(skeleton[None], 'row', axis=0, tiled=True)]
    ppermute x9 -> x0, waiting for transfers between devices: 13.9 us -> none  [the longest x5 12.8 us: partner_2(): return lax.ppermute(block, axis, route)]
    dot_general x28 -> x0, matrix products: 13.4 us -> none  [the longest x1 3.46 us: tendency(): jnp.einsum('ik,fkjrc->fijrc', derivative, values, precision=full_precision)]
    slice x14 -> x0, local copies, waits for them, and re-layouts: 12.8 us -> none  [the longest x2 6.02 us: extended(): last = lax.slice_in_dim(x, length - width, length, axis=dim)]
    unnamed x34 -> x31, local copies, waits for them, and re-layouts: 3.93 us -> 14.9 us
    ppermute x2 -> x0, local copies, waits for them, and re-layouts: 9.2 us -> none  [the longest x1 4.6 us: extended(): before = lax.ppermute(last, axis, up)]
  transfers between devices with their start and end apart: 9 -> 0, of which waited for: 7 -> 0; matrix products, arithmetic and copies ran while one was open for 9% -> 0% of each run, Pallas kernels for 0% -> 0%
where the time goes in v1:
time: 51.6 us; the launch traced here: 50.9 us
  Pallas kernels  36 us (70%)
  local copies, waits for them, and re-layouts  14.9 us (29%)
    pallas_call x1, Pallas kernels, local(): pl.pallas_call(kernel, name='imex_step', out_shape=jax.ShapeDtypeStruct((...  36 us
    unnamed x31, local copies, waits for them, and re-layouts  14.9 us

profile of v1, /device:TPU:1, one launch (start us, length us, event | category | flops | bytes accessed | tf_op | source)
XLA Modules:
  0.0 50.9 jit_solution(17346475959292033627)
XLA Ops:
  0.0 0.0 copy-start
  0.0 1.2 %copy-done = f32[2048,128]{1,0:T(8,128)S(1)} copy-done((f32[2048,128]{1,0:T(8,128)S(1)}, f32[2048,128]{1,0:T(8,128)}, u32[]{:S(2)}) %copy-start) | copy-done | bytes 1048600
  1.2 0.0 copy-start.1
  1.2 1.1 %copy-done.1 = f32[5,256,128]{2,1,0:T(8,128)S(1)} copy-done((f32[5,256,128]{2,1,0:T(8,128)S(1)}, f32[5,256,128]{2,1,0:T(8,128)}, u32[]{:S(2)}) %copy-start.1) | copy-done | bytes 655384
  2.3 0.0 copy-start.2
  2.3 1.1 %copy-done.2 = f32[5,128,256]{2,1,0:T(8,128)S(1)} copy-done((f32[5,128,256]{2,1,0:T(8,128)S(1)}, f32[5,128,256]{2,1,0:T(8,128)}, u32[]{:S(2)}) %copy-start.2) | copy-done | bytes 655384
  3.4 0.0 copy-start.3
  3.4 1.0 %copy-done.3 = bf16[4,16,16,1,1,256]{5,2,4,3,1,0:T(8,128)(2,1)S(1)} copy-done((bf16[4,16,16,1,1,256]{5,2,4,3,1,0:T(8,128)(2,1)S(1)}, bf16[4,16,16,1,1,256]{5,2,4,3,1,0:T(8,128)(2,1)}, u32[]{:S(2)}) %copy-start.3) | copy-done | bytes 524312
  4.4 0.0 copy-start.4
  4.4 1.0 %copy-done.4 = f32[5,128,128]{2,1,0:T(8,128)S(1)} copy-done((f32[5,128,128]{2,1,0:T(8,128)S(1)}, f32[5,128,128]{2,1,0:T(8,128)}, u32[]{:S(2)}) %copy-start.4) | copy-done | bytes 327704
  5.4 0.0 copy-start.5
  5.4 0.9 %copy-done.5 = f32[256,256]{1,0:T(8,128)S(1)} copy-done((f32[256,256]{1,0:T(8,128)S(1)}, f32[256,256]{1,0:T(8,128)}, u32[]{:S(2)}) %copy-start.5) | copy-done | bytes 262168
  6.4 0.0 copy-start.6
  6.4 0.9 %copy-done.6 = bf16[512,256]{1,0:T(8,128)(2,1)S(1)} copy-done((bf16[512,256]{1,0:T(8,128)(2,1)S(1)}, bf16[512,256]{1,0:T(8,128)(2,1)}, u32[]{:S(2)}) %copy-start.6) | copy-done | bytes 262168
  7.3 0.0 copy-start.7
  7.3 0.9 %copy-done.7 = bf16[512,256]{1,0:T(8,128)(2,1)S(1)} copy-done((bf16[512,256]{1,0:T(8,128)(2,1)S(1)}, bf16[512,256]{1,0:T(8,128)(2,1)}, u32[]{:S(2)}) %copy-start.7) | copy-done | bytes 262168
  8.3 0.0 copy-start.8
  8.3 0.9 %copy-done.8 = f32[256,128]{1,0:T(8,128)S(1)} copy-done((f32[256,128]{1,0:T(8,128)S(1)}, f32[256,128]{1,0:T(8,128)}, u32[]{:S(2)}) %copy-start.8) | copy-done | bytes 131096
  9.2 0.0 copy-start.9
  9.2 0.9 %copy-done.9 = f32[256,128]{1,0:T(8,128)S(1)} copy-done((f32[256,128]{1,0:T(8,128)S(1)}, f32[256,128]{1,0:T(8,128)}, u32[]{:S(2)}) %copy-start.9) | copy-done | bytes 131096
  10.1 0.0 copy-start.10
  10.1 0.8 %copy-done.10 = f32[64,256]{1,0:T(8,128)S(1)} copy-done((f32[64,256]{1,0:T(8,128)S(1)}, f32[64,256]{1,0:T(8,128)}, u32[]{:S(2)}) %copy-start.10) | copy-done | bytes 65560
  10.9 0.0 copy-start.11
  10.9 0.8 %copy-done.11 = f32[256,64]{0,1:T(8,128)S(1)} copy-done((f32[256,64]{0,1:T(8,128)S(1)}, f32[256,64]{0,1:T(8,128)}, u32[]{:S(2)}) %copy-start.11) | copy-done | bytes 65560
  11.8 0.0 copy-start.12
  11.8 0.8 %copy-done.12 = bf16[256,64]{1,0:T(8,128)(2,1)S(1)} copy-done((bf16[256,64]{1,0:T(8,128)(2,1)S(1)}, bf16[256,64]{1,0:T(8,128)(2,1)}, u32[]{:S(2)}) %copy-start.12) | copy-done | bytes 32792
  12.6 0.0 copy-start.13
  12.6 0.8 %copy-done.13 = f32[64,128]{1,0:T(8,128)S(1)} copy-done((f32[64,128]{1,0:T(8,128)S(1)}, f32[64,128]{1,0:T(8,128)}, u32[]{:S(2)}) %copy-start.13) | copy-done | bytes 32792
  13.4 0.0 copy-start.14
  13.4 0.8 %copy-done.14 = f32[64,128]{1,0:T(8,128)S(1)} copy-done((f32[64,128]{1,0:T(8,128)S(1)}, f32[64,128]{1,0:T(8,128)}, u32[]{:S(2)}) %copy-start.14) | copy-done | bytes 32792
  14.1 36.0 %imex_step.1 = bf16[1024,256]{1,0:T(8,128)(2,1)S(1)} custom-call(bf16[1024,256]{1,0:T(8,128)(2,1)S(1)} %bitcast.6, f32[256,256]{1,0:T(8,128)S(1)} %copy-done.5, f32[64,256]{1,0:T(8,128)S(1)} %copy-done.10, f32[64,128]{1,0:T(8,128)S(1)} %copy-done.13, f32[256,128]{1,0:T(8,128)S(1)} %copy-done.8, f32[5,128,128]{2,1,0:T(8,128)S(1)} %copy-done.4, ...), custom_call_target="tpu_custom_call" | custom-call | tf_op jit(solution)/shard_map/imex_step/pallas_call | solution.py:274
  50.1 0.8 %copy.18 = bf16[4,16,16,1,1,256]{5,2,4,3,1,0:T(8,128)(2,1)} copy(bf16[4,16,16,1,1,256]{5,2,4,3,1,0:T(8,128)(2,1)S(1)} %bitcast.5) | data formatting | bytes 1048576
Async XLA Ops:
  0.0 1.2 %copy-start = (f32[2048,128]{1,0:T(8,128)S(1)}, f32[2048,128]{1,0:T(8,128)}, u32[]{:S(2)}) copy-start(f32[2048,128]{1,0:T(8,128)} %top_ref.1) | copy-start | bytes 3145732
  1.2 1.1 %copy-start.1 = (f32[5,256,128]{2,1,0:T(8,128)S(1)}, f32[5,256,128]{2,1,0:T(8,128)}, u32[]{:S(2)}) copy-start(f32[5,256,128]{2,1,0:T(8,128)} %parent_ref.1) | copy-start | bytes 1966084
  2.3 1.1 %copy-start.2 = (f32[5,128,256]{2,1,0:T(8,128)S(1)}, f32[5,128,256]{2,1,0:T(8,128)}, u32[]{:S(2)}) copy-start(f32[5,128,256]{2,1,0:T(8,128)} %child_ref.1) | copy-start | bytes 1966084
  3.4 1.0 %copy-start.3 = (bf16[4,16,16,1,1,256]{5,2,4,3,1,0:T(8,128)(2,1)S(1)}, bf16[4,16,16,1,1,256]{5,2,4,3,1,0:T(8,128)(2,1)}, u32[]{:S(2)}) copy-start(bf16[4,16,16,1,1,256]{5,2,4,3,1,0:T(8,128)(2,1)} %param.15) | copy-start | bytes 1572868
  4.4 1.0 %copy-start.4 = (f32[5,128,128]{2,1,0:T(8,128)S(1)}, f32[5,128,128]{2,1,0:T(8,128)}, u32[]{:S(2)}) copy-start(f32[5,128,128]{2,1,0:T(8,128)} %mi_ref.1) | copy-start | bytes 983044
  5.4 0.9 %copy-start.5 = (f32[256,256]{1,0:T(8,128)S(1)}, f32[256,256]{1,0:T(8,128)}, u32[]{:S(2)}) copy-start(f32[256,256]{1,0:T(8,128)} %solve_ref.1) | copy-start | bytes 786436
  6.4 0.9 %copy-start.6 = (bf16[512,256]{1,0:T(8,128)(2,1)S(1)}, bf16[512,256]{1,0:T(8,128)(2,1)}, u32[]{:S(2)}) copy-start(bf16[512,256]{1,0:T(8,128)(2,1)} %constant.7.clone.der_l_ref) | copy-start | bytes 786436
  7.3 0.9 %copy-start.7 = (bf16[512,256]{1,0:T(8,128)(2,1)S(1)}, bf16[512,256]{1,0:T(8,128)(2,1)}, u32[]{:S(2)}) copy-start(bf16[512,256]{1,0:T(8,128)(2,1)} %constant.6.clone.der_h_ref) | copy-start | bytes 786436
  8.3 0.9 %copy-start.8 = (f32[256,128]{1,0:T(8,128)S(1)}, f32[256,128]{1,0:T(8,128)}, u32[]{:S(2)}) copy-start(f32[256,128]{1,0:T(8,128)} %lift_l_ref.1) | copy-start | bytes 393220
  9.2 0.9 %copy-start.9 = (f32[256,128]{1,0:T(8,128)S(1)}, f32[256,128]{1,0:T(8,128)}, u32[]{:S(2)}) copy-start(f32[256,128]{1,0:T(8,128)} %spr_l_ref.1) | copy-start | bytes 393220
  10.1 0.8 %copy-start.10 = (f32[64,256]{1,0:T(8,128)S(1)}, f32[64,256]{1,0:T(8,128)}, u32[]{:S(2)}) copy-start(f32[64,256]{1,0:T(8,128)} %flux_ref.1) | copy-start | bytes 196612
  10.9 0.8 %copy-start.11 = (f32[256,64]{0,1:T(8,128)S(1)}, f32[256,64]{0,1:T(8,128)}, u32[]{:S(2)}) copy-start(f32[256,64]{0,1:T(8,128)} %param.26) | copy-start | bytes 196612
  11.8 0.8 %copy-start.12 = (bf16[256,64]{1,0:T(8,128)(2,1)S(1)}, bf16[256,64]{1,0:T(8,128)(2,1)}, u32[]{:S(2)}) copy-start(bf16[256,64]{1,0:T(8,128)(2,1)} %constant.8.clone.face_ref) | copy-start | bytes 98308
  12.6 0.8 %copy-start.13 = (f32[64,128]{1,0:T(8,128)S(1)}, f32[64,128]{1,0:T(8,128)}, u32[]{:S(2)}) copy-start(f32[64,128]{1,0:T(8,128)} %lift_e_ref.1) | copy-start | bytes 98308
  13.4 0.8 %copy-start.14 = (f32[64,128]{1,0:T(8,128)S(1)}, f32[64,128]{1,0:T(8,128)}, u32[]{:S(2)}) copy-start(f32[64,128]{1,0:T(8,128)} %spr_e_ref.1) | copy-start | bytes 98308

commit v2 on v1

--- a/solution.py
+++ b/solution.py
@@ -63,10 +63,13 @@
     return sum(((m >> k) & 1) << (LEVELS - 1 - k) for k in range(LEVELS))
 
 
-def kernel(
-    q_ref, solve_ref, flux_ref, lift_e_ref, lift_l_ref, mi_ref, parent_ref, child_ref, top_ref,
-    spr_e_ref, spr_l_ref, ext_t_ref, der_h_ref, der_l_ref, face_ref,
-    out_ref,
+def kernel(*refs):
+    stored, out_ref, held, loaded = refs[:15], refs[15], refs[16:31], refs[31]
+    step(stored, held, loaded, out_ref, *refs[32:])
+
+
+def step(
+    stored, held, loaded, out_ref,
     tend_ref, part_ref, k_ref, src1, dst1, src2, dst2, src3, dst3, src4, dst4,
     par_h, par_l, top_h, top_l,
     send1, recv1, send2, recv2, send3, recv3, send4, recv4,
@@ -89,6 +92,21 @@
     for d in range(1, N_ROW):
         pl.semaphore_signal(barrier, inc=1, device_id=(row_at(d), col), device_id_type=MESH)
 
+    (
+        q_ref, solve_ref, flux_ref, lift_e_ref, lift_l_ref, mi_ref, parent_ref, child_ref,
+        top_ref, spr_e_ref, spr_l_ref, ext_t_ref, der_h_ref, der_l_ref, face_ref,
+    ) = held
+    loads = [
+        pltpu.make_async_copy(stored[i], held[i], loaded.at[i]) for i in range(15)
+    ]
+    for i in (0, 12, 13, 2, 3, 4, 6, 1, 14, 5, 7, 8, 11, 9, 10):
+        loads[i].start()
+
+    def arrived(*which):
+        for i in which:
+            loads[i].wait()
+
+    arrived(0, 12, 13)
     der_h, der_l = der_h_ref[...], der_l_ref[...]
     q0 = q_ref[0:256, :].astype(F32)
     q1 = q_ref[256:512, :].astype(F32)
@@ -127,6 +145,7 @@
     south.start()
     north.start()
 
+    arrived(2, 3, 4)
     k_map = dot3(
         split(flux_ref[...].T), split(lift_e_ref[...])
     )
@@ -162,6 +181,7 @@
     east.start()
     west.start()
 
+    arrived(6)
     for k in range(LEVELS):
         whole = parent_ref[k]
         swapped = jnp.concatenate([whole[128:], whole[:128]], axis=0)
@@ -205,6 +225,7 @@
     for copy in gathers:
         copy.start()
 
+    arrived(1, 14)
     solve = split(solve_ref[...])
     face = face_ref[...]
     solve_face = (mm(solve[0], face).astype(BF16), mm(solve[1], face).astype(BF16))
@@ -214,6 +235,7 @@
         part_ref[256 * f : 256 * f + 256, :] = dot3(
             solve, split(q - tend_ref[256 * f : 256 * f + 256, :])
         ) - dot3(solve_face, split(change))
+    arrived(5, 7, 8)
     chain = None
     interface_maps = []
     for k in range(LEVELS):
@@ -228,6 +250,7 @@
         high, low = split(dot3(split(top_ref[at, :]), chain))
         top_h[at, :] = high
         top_l[at, :] = low
+    arrived(11, 9, 10)
     extend = dot3(split(ext_t_ref[...].T), split(spr_e_ref[...]))
     spread_l = split(spr_l_ref[...])
 
@@ -271,13 +294,20 @@
 ):
     der_h, der_l = derivative_parts()
     dma = pltpu.SemaphoreType.DMA
+    args = (
+        state_fields.reshape(1024, 256), leaf_solve, leaf_flux, lift_edges, lift_leaves,
+        merge_interface, merge_parent, split_child, top_inverse, spread_edges, spread_leaves,
+        leaf_extend.T, jnp.asarray(der_h), jnp.asarray(der_l), jnp.asarray(face_columns()),
+    )
     result = pl.pallas_call(
         kernel,
         name="imex_step",
         out_shape=jax.ShapeDtypeStruct((1024, 256), BF16),
-        in_specs=[pl.BlockSpec(memory_space=pltpu.VMEM)] * 15,
+        in_specs=[pl.BlockSpec(memory_space=pltpu.HBM)] * 15,
         out_specs=pl.BlockSpec(memory_space=pltpu.VMEM),
-        scratch_shapes=[
+        scratch_shapes=[pltpu.VMEM(a.shape, a.dtype) for a in args]
+        + [
+            dma((15,)),
             pltpu.VMEM((1024, 256), F32),
             pltpu.VMEM((1024, 256), F32),
             pltpu.VMEM((256, 128), F32),
@@ -297,13 +327,9 @@
             dma((N_COL,)), dma((N_COL,)), dma((N_ROW,)), dma((N_ROW,)),
         ],
         compiler_params=pltpu.CompilerParams(
-            collective_id=0, has_side_effects=True, vmem_limit_bytes=48 * 1024 * 1024
+            collective_id=0, has_side_effects=True, vmem_limit_bytes=67043328
         ),
-    )(
-        state_fields.reshape(1024, 256), leaf_solve, leaf_flux, lift_edges, lift_leaves,
-        merge_interface, merge_parent, split_child, top_inverse, spread_edges, spread_leaves,
-        leaf_extend.T, jnp.asarray(der_h), jnp.asarray(der_l), jnp.asarray(face_columns()),
-    )
+    )(*args)
     return result.reshape(state_fields.shape)
 
 

time: 51.6 us -> 38.9 us (0.75); the launches traced: 50.9 us -> 38.8 us
  local copies, waits for them, and re-layouts: 14.9 us -> 1.87 us
  Pallas kernels: 36 us -> 36.9 us
    unnamed x31 -> x1, local copies, waits for them, and re-layouts: 14.9 us -> 1.87 us
    pallas_call x1, Pallas kernels: 36 us -> 36.9 us  [local(): pl.pallas_call(kernel, name='imex_step', out_shape=jax.ShapeDtypeStruct((...]
where the time goes in v2:
time: 38.9 us; the launch traced here: 38.8 us
  Pallas kernels  36.9 us (95%)
  local copies, waits for them, and re-layouts  1.87 us (5%)
    pallas_call x1, Pallas kernels, local(): pl.pallas_call(kernel, name='imex_step', out_shape=jax.ShapeDtypeStruct((...  36.9 us
    unnamed x1, local copies, waits for them, and re-layouts  1.87 us

profile of v2, /device:TPU:1, one launch (start us, length us, event | category | flops | bytes accessed | tf_op | source)
XLA Modules:
  0.0 38.8 jit_solution(4704438568488207086)
XLA Ops:
  0.0 36.9 %imex_step.1 = bf16[1024,256]{1,0:T(8,128)(2,1)} custom-call(bf16[1024,256]{1,0:T(8,128)(2,1)} %bitcast.6, f32[256,256]{1,0:T(8,128)} %refs_1_.1, f32[64,256]{1,0:T(8,128)} %refs_2_.1, f32[64,128]{1,0:T(8,128)} %refs_3_.1, f32[256,128]{1,0:T(8,128)} %refs_4_.1, f32[5,128,128]{2,1,0:T(8,128)} %refs_5_.1, f32[5,256,128]{2,1,0:T(8,128)} %refs_6_.1, ...), custom_call_target="tpu_custom_call" | custom-call | tf_op jit(solution)/shard_map/imex_step/pallas_call | solution.py:302
  36.9 1.9 %copy.18 = bf16[4,16,16,1,1,256]{5,2,4,3,1,0:T(8,128)(2,1)} copy(bf16[4,16,16,1,1,256]{5,2,4,3,1,0:T(8,128)(2,1)} %bitcast.5) | data formatting | bytes 1048576

commit v3 on v2

--- a/solution.py
+++ b/solution.py
@@ -59,6 +59,13 @@
     return mm(a[0], b[0], dims) + mm(a[0], b[1], dims) + mm(a[1], b[0], dims)
 
 
+def few_rows_dot3(a, b):
+    high = a.astype(BF16)
+    rows = a.shape[0]
+    both = mm(jnp.concatenate([a, a - high.astype(F32)], axis=0).astype(BF16), b[0])
+    return both[:rows] + both[rows:] + mm(high, b[1])
+
+
 def bit_reversed(m):
     return sum(((m >> k) & 1) << (LEVELS - 1 - k) for k in range(LEVELS))
 
@@ -86,12 +93,6 @@
     def row_at(d):
         return (row + d) % N_ROW
 
-    barrier = pltpu.get_barrier_semaphore()
-    for m in range(1, N_COL):
-        pl.semaphore_signal(barrier, inc=1, device_id=(row, other(m)), device_id_type=MESH)
-    for d in range(1, N_ROW):
-        pl.semaphore_signal(barrier, inc=1, device_id=(row_at(d), col), device_id_type=MESH)
-
     (
         q_ref, solve_ref, flux_ref, lift_e_ref, lift_l_ref, mi_ref, parent_ref, child_ref,
         top_ref, spr_e_ref, spr_l_ref, ext_t_ref, der_h_ref, der_l_ref, face_ref,
@@ -101,6 +102,12 @@
     ]
     for i in (0, 12, 13, 2, 3, 4, 6, 1, 14, 5, 7, 8, 11, 9, 10):
         loads[i].start()
+
+    barrier = pltpu.get_barrier_semaphore()
+    for m in range(1, N_COL):
+        pl.semaphore_signal(barrier, inc=1, device_id=(row, other(m)), device_id_type=MESH)
+    for d in range(1, N_ROW):
+        pl.semaphore_signal(barrier, inc=1, device_id=(row_at(d), col), device_id_type=MESH)
 
     def arrived(*which):
         for i in which:
@@ -252,10 +259,11 @@
         top_l[at, :] = low
     arrived(11, 9, 10)
     extend = dot3(split(ext_t_ref[...].T), split(spr_e_ref[...]))
-    spread_l = split(spr_l_ref[...])
+    spread_h, spread_low = split(spr_l_ref[...])
+    spread_twice = jnp.concatenate([spread_h, spread_h], axis=1)
 
     for copy in gathers:
-        copy.wait()
+        copy.wait_recv()
     x = dst3[...].reshape(4 * N_COL, 128)
     differences = []
     for k in range(LEVELS):
@@ -263,7 +271,7 @@
         first, second = x[:rows], x[rows:]
         differences.append((second - first)[:4])
         joined = jnp.concatenate([first, second], axis=1)
-        x = dot3(split(joined), (par_h[k], par_l[k]))
+        x = few_rows_dot3(joined, (par_h[k], par_l[k]))
     src4[...] = x
     dst4[row] = x
     sends = []
@@ -275,17 +283,19 @@
         )
     for copy in sends:
         copy.start()
-    boundary = dot3(split(jnp.concatenate(differences, axis=1)), interface_map)
-    for copy in sends:
+    boundary = few_rows_dot3(jnp.concatenate(differences, axis=1), interface_map)
+    for copy in gathers + sends:
         copy.wait_send()
     for copy in arrivals:
         copy.wait_recv()
-    pieces = split(jnp.concatenate([dst4[g] for g in range(N_ROW)], axis=1))
-    boundary = boundary + dot3(pieces, (top_h[...], top_l[...]))
+    pieces = jnp.concatenate([dst4[g] for g in range(N_ROW)], axis=1)
+    boundary = boundary + few_rows_dot3(pieces, (top_h[...], top_l[...]))
     for f in range(4):
         weighted = split(extend * boundary[f : f + 1, :])
         at = slice(256 * f, 256 * f + 256)
-        out_ref[at, :] = (part_ref[at, :] + dot3(weighted, spread_l, ((1,), (1,)))).astype(BF16)
+        edges = mm(jnp.concatenate(weighted, axis=1), spread_twice, ((1,), (1,)))
+        edges = edges + mm(weighted[0], spread_low, ((1,), (1,)))
+        out_ref[at, :] = (part_ref[at, :] + edges).astype(BF16)
 
 
 def local(
@@ -327,9 +337,9 @@
             dma((N_COL,)), dma((N_COL,)), dma((N_ROW,)), dma((N_ROW,)),
         ],
         compiler_params=pltpu.CompilerParams(
-            collective_id=0, has_side_effects=True, vmem_limit_bytes=67043328
+            collective_id=0, has_side_effects=True, vmem_limit_bytes=48 * 1024 * 1024
         ),
-    )(*args)
+    )(*[pltpu.with_memory_space_constraint(a, pltpu.HBM) for a in args])
     return result.reshape(state_fields.shape)
 
 

time: 38.9 us -> 36.8 us (0.946)
  local copies, waits for them, and re-layouts: 1.87 us -> 0.8 us
  Pallas kernels: 36.9 us -> 35.9 us
    unnamed x1, local copies, waits for them, and re-layouts: 1.87 us -> 0.8 us
    pallas_call x1, Pallas kernels: 36.9 us -> 35.9 us  [local(): pl.pallas_call(kernel, name='imex_step', out_shape=jax.ShapeDtypeStruct((...]
where the time goes in v3:
time: 36.8 us; the launch traced here: 36.7 us
  Pallas kernels  35.9 us (98%)
  local copies, waits for them, and re-layouts  0.8 us (2%)
    pallas_call x1, Pallas kernels, local(): pl.pallas_call(kernel, name='imex_step', out_shape=jax.ShapeDtypeStruct((...  35.9 us
    unnamed x1, local copies, waits for them, and re-layouts  0.8 us

profile of v3, /device:TPU:1, one launch (start us, length us, event | category | flops | bytes accessed | tf_op | source)
XLA Modules:
  0.0 36.7 jit_solution(15744544250024617716)
XLA Ops:
  0.0 35.9 %imex_step.1 = bf16[1024,256]{1,0:T(8,128)(2,1)S(1)} custom-call(bf16[1024,256]{1,0:T(8,128)(2,1)} %bitcast.6, f32[256,256]{1,0:T(8,128)} %refs_1_.1, f32[64,256]{1,0:T(8,128)} %refs_2_.1, f32[64,128]{1,0:T(8,128)} %refs_3_.1, f32[256,128]{1,0:T(8,128)} %refs_4_.1, f32[5,128,128]{2,1,0:T(8,128)} %refs_5_.1, f32[5,256,128]{2,1,0:T(8,128)} %refs_6_.1, ...), custom_call_target="tpu_custom_call" | custom-call | tf_op jit(solution)/shard_map/imex_step/pallas_call | solution.py:312
  35.9 0.8 %copy.18 = bf16[4,16,16,1,1,256]{5,2,4,3,1,0:T(8,128)(2,1)} copy(bf16[4,16,16,1,1,256]{5,2,4,3,1,0:T(8,128)(2,1)S(1)} %bitcast.5) | data formatting | bytes 1048576

commit v4 on v3

--- a/solution.py
+++ b/solution.py
@@ -12,6 +12,10 @@
 LEVELS = 5
 N_ROW = 16
 N_COL = 32
+LOW = 3
+HIGH = LEVELS - LOW
+NEAR = [m for m in range(7, 0, -1)]
+FAR = [m << LOW for m in range(3, 0, -1)]
 advect_scale = 0.01
 
 
@@ -66,8 +70,8 @@
     return both[:rows] + both[rows:] + mm(high, b[1])
 
 
-def bit_reversed(m):
-    return sum(((m >> k) & 1) << (LEVELS - 1 - k) for k in range(LEVELS))
+def bit_reversed(m, width):
+    return sum(((m >> k) & 1) << (width - 1 - k) for k in range(width))
 
 
 def kernel(*refs):
@@ -77,9 +81,9 @@
 
 def step(
     stored, held, loaded, out_ref,
-    tend_ref, part_ref, k_ref, src1, dst1, src2, dst2, src3, dst3, src4, dst4,
+    tend_ref, part_ref, k_ref, src1, dst1, src2, dst2, src3, dst3, src4, dst4, src5, dst5,
     par_h, par_l, top_h, top_l,
-    send1, recv1, send2, recv2, send3, recv3, send4, recv4,
+    send1, recv1, send2, recv2, send3, recv3, send4, recv4, send5, recv5,
 ):
     row = lax.axis_index("row")
     col = lax.axis_index("col")
@@ -104,10 +108,11 @@
         loads[i].start()
 
     barrier = pltpu.get_barrier_semaphore()
-    for m in range(1, N_COL):
-        pl.semaphore_signal(barrier, inc=1, device_id=(row, other(m)), device_id_type=MESH)
-    for d in range(1, N_ROW):
-        pl.semaphore_signal(barrier, inc=1, device_id=(row_at(d), col), device_id_type=MESH)
+    peers = [(row_at(d), col) for d in (8, 7, 9, 6, 10, 5, 11, 4, 12, 3, 13, 2, 14, 1, 15)]
+    peers += [(row, other(m)) for m in NEAR + FAR]
+    peers += [(row, (col + 1) % N_COL), (row, (col + N_COL - 1) % N_COL)]
+    for peer in peers:
+        pl.semaphore_signal(barrier, inc=1, device_id=peer, device_id_type=MESH)
 
     def arrived(*which):
         for i in which:
@@ -139,7 +144,7 @@
     below = pltpu.roll(top, 192, 1)
     src1[0] = above[:, :128]
     src1[1] = below[:, 128:]
-    pl.semaphore_wait(barrier, N_COL - 1 + N_ROW - 1)
+    pl.semaphore_wait(barrier, len(peers))
 
     def remote(src, dst, send, recv, where):
         return pltpu.make_async_remote_copy(
@@ -223,12 +228,10 @@
     skeleton = jnp.concatenate(skeleton, axis=0)
     src3[...] = skeleton
     dst3[0] = skeleton
-    gathers = []
-    for m in range(N_COL - 1, 0, -1):
-        slot = bit_reversed(m)
-        gathers.append(
-            remote(src3, dst3.at[slot], send3.at[m], recv3.at[m], (row, other(m)))
-        )
+    gathers = [
+        remote(src3, dst3.at[bit_reversed(m, LOW)], send3.at[m], recv3.at[m], (row, other(m)))
+        for m in NEAR
+    ]
     for copy in gathers:
         copy.start()
 
@@ -242,6 +245,32 @@
         part_ref[256 * f : 256 * f + 256, :] = dot3(
             solve, split(q - tend_ref[256 * f : 256 * f + 256, :])
         ) - dot3(solve_face, split(change))
+    for copy in gathers:
+        copy.wait_recv()
+    differences = []
+
+    def merged(x, level):
+        rows = x.shape[0] // 2
+        first, second = x[:rows], x[rows:]
+        differences.append((second - first)[:4])
+        joined = jnp.concatenate([first, second], axis=1)
+        return few_rows_dot3(joined, (par_h[level], par_l[level]))
+
+    x = dst3[...].reshape(4 << LOW, 128)
+    for k in range(LOW):
+        x = merged(x, k)
+    src5[...] = x
+    dst5[0] = x
+    crossings = [
+        remote(
+            src5, dst5.at[bit_reversed(m >> LOW, HIGH)], send5.at[m >> LOW], recv5.at[m >> LOW],
+            (row, other(m)),
+        )
+        for m in FAR
+    ]
+    for copy in crossings:
+        copy.start()
+
     arrived(5, 7, 8)
     chain = None
     interface_maps = []
@@ -262,16 +291,11 @@
     spread_h, spread_low = split(spr_l_ref[...])
     spread_twice = jnp.concatenate([spread_h, spread_h], axis=1)
 
-    for copy in gathers:
+    for copy in crossings:
         copy.wait_recv()
-    x = dst3[...].reshape(4 * N_COL, 128)
-    differences = []
-    for k in range(LEVELS):
-        rows = (4 * N_COL) >> (k + 1)
-        first, second = x[:rows], x[rows:]
-        differences.append((second - first)[:4])
-        joined = jnp.concatenate([first, second], axis=1)
-        x = few_rows_dot3(joined, (par_h[k], par_l[k]))
+    x = dst5[...].reshape(4 << HIGH, 128)
+    for k in range(LOW, LEVELS):
+        x = merged(x, k)
     src4[...] = x
     dst4[row] = x
     sends = []
@@ -284,7 +308,7 @@
     for copy in sends:
         copy.start()
     boundary = few_rows_dot3(jnp.concatenate(differences, axis=1), interface_map)
-    for copy in gathers + sends:
+    for copy in gathers + crossings + sends:
         copy.wait_send()
     for copy in arrivals:
         copy.wait_recv()
@@ -326,15 +350,18 @@
             pltpu.VMEM((2, 64, 128), F32),
             pltpu.VMEM((2, 64, 128), F32),
             pltpu.VMEM((4, 128), F32),
-            pltpu.VMEM((N_COL, 4, 128), F32),
+            pltpu.VMEM((1 << LOW, 4, 128), F32),
             pltpu.VMEM((4, 128), F32),
             pltpu.VMEM((N_ROW, 4, 128), F32),
+            pltpu.VMEM((4, 128), F32),
+            pltpu.VMEM((1 << HIGH, 4, 128), F32),
             pltpu.VMEM((LEVELS, 256, 128), BF16),
             pltpu.VMEM((LEVELS, 256, 128), BF16),
             pltpu.VMEM((2048, 128), BF16),
             pltpu.VMEM((2048, 128), BF16),
             dma((2,)), dma((2,)), dma((2,)), dma((2,)),
-            dma((N_COL,)), dma((N_COL,)), dma((N_ROW,)), dma((N_ROW,)),
+            dma((1 << LOW,)), dma((1 << LOW,)), dma((N_ROW,)), dma((N_ROW,)),
+            dma((1 << HIGH,)), dma((1 << HIGH,)),
         ],
         compiler_params=pltpu.CompilerParams(
             collective_id=0, has_side_effects=True, vmem_limit_bytes=48 * 1024 * 1024

time: 36.8 us -> 38 us (1.033)
  Pallas kernels: 35.9 us -> 37.1 us
    pallas_call x1, Pallas kernels: 35.9 us -> 37.1 us  [local(): pl.pallas_call(kernel, name='imex_step', out_shape=jax.ShapeDtypeStruct((...]
where the time goes in v4:
time: 38 us; the launch traced here: 37.9 us
  Pallas kernels  37.1 us (98%)
  local copies, waits for them, and re-layouts  0.8 us (2%)
    pallas_call x1, Pallas kernels, local(): pl.pallas_call(kernel, name='imex_step', out_shape=jax.ShapeDtypeStruct((...  37.1 us
    unnamed x1, local copies, waits for them, and re-layouts  0.8 us

profile of v4, /device:TPU:1, one launch (start us, length us, event | category | flops | bytes accessed | tf_op | source)
XLA Modules:
  0.0 37.9 jit_solution(17219646809630341233)
XLA Ops:
  0.0 37.1 %imex_step.1 = bf16[1024,256]{1,0:T(8,128)(2,1)S(1)} custom-call(bf16[1024,256]{1,0:T(8,128)(2,1)} %bitcast.6, f32[256,256]{1,0:T(8,128)} %refs_1_.1, f32[64,256]{1,0:T(8,128)} %refs_2_.1, f32[64,128]{1,0:T(8,128)} %refs_3_.1, f32[256,128]{1,0:T(8,128)} %refs_4_.1, f32[5,128,128]{2,1,0:T(8,128)} %refs_5_.1, f32[5,256,128]{2,1,0:T(8,128)} %refs_6_.1, ...), custom_call_target="tpu_custom_call" | custom-call | tf_op jit(solution)/shard_map/imex_step/pallas_call | solution.py:336
  37.1 0.8 %copy.18 = bf16[4,16,16,1,1,256]{5,2,4,3,1,0:T(8,128)(2,1)} copy(bf16[4,16,16,1,1,256]{5,2,4,3,1,0:T(8,128)(2,1)S(1)} %bitcast.5) | data formatting | bytes 1048576

commit v5 on v3

--- a/solution.py
+++ b/solution.py
@@ -77,9 +77,9 @@
 
 def step(
     stored, held, loaded, out_ref,
-    tend_ref, part_ref, k_ref, src1, dst1, src2, dst2, src3, dst3, src4, dst4,
+    tend_ref, part_ref, k_ref, src1, dst1, src2, dst2, src3, dst3, src4, dst4, src6, dst6,
     par_h, par_l, top_h, top_l,
-    send1, recv1, send2, recv2, send3, recv3, send4, recv4,
+    send1, recv1, send2, recv2, send3, recv3, send4, recv4, send6, recv6,
 ):
     row = lax.axis_index("row")
     col = lax.axis_index("col")
@@ -108,6 +108,11 @@
         pl.semaphore_signal(barrier, inc=1, device_id=(row, other(m)), device_id_type=MESH)
     for d in range(1, N_ROW):
         pl.semaphore_signal(barrier, inc=1, device_id=(row_at(d), col), device_id_type=MESH)
+    down, up = row_at(1), row_at(N_ROW - 1)
+    east_col, west_col = (col + 1) % N_COL, (col + N_COL - 1) % N_COL
+    diagonal = [(down, east_col), (down, west_col), (up, east_col), (up, west_col)]
+    for peer in diagonal:
+        pl.semaphore_signal(barrier, inc=1, device_id=peer, device_id_type=MESH)
 
     def arrived(*which):
         for i in which:
@@ -139,7 +144,35 @@
     below = pltpu.roll(top, 192, 1)
     src1[0] = above[:, :128]
     src1[1] = below[:, 128:]
-    pl.semaphore_wait(barrier, N_COL - 1 + N_ROW - 1)
+
+    left, right = nodes_of(0), nodes_of(15)
+
+    def with_corners(top_rows, bottom_rows):
+        left_rows = jnp.where(
+            place == 0, top_rows, jnp.where(place == 15, pltpu.roll(bottom_rows, 15, 0), left)
+        )
+        right_rows = jnp.where(
+            place == 0, pltpu.roll(top_rows, 49, 0), jnp.where(place == 15, bottom_rows, right)
+        )
+        return left_rows, right_rows
+
+    left_part, right_part = with_corners(
+        (top + jnp.where(lane < 64, 0.0, above)) * 0.5,
+        (bottom + jnp.where(lane >= 192, 0.0, below)) * 0.5,
+    )
+    to_east = pltpu.roll(right_part, 193, 1)
+    to_west = pltpu.roll(left_part, 63, 1)
+    src2[0] = jnp.where(half_lane % 64 == 0, to_east[:, :128], pltpu.roll(to_east[:, 128:], 1, 1))
+    src2[1] = jnp.where(half_lane % 64 == 63, to_west[:, :128], pltpu.roll(to_west[:, 128:], 1, 1))
+
+    def corner(rows, shift, node):
+        return pltpu.roll(rows, shift, 1).reshape(4, 16, 128)[:, node, :]
+
+    src6[0] = corner(above[:, :128], 65, 15)
+    src6[1] = corner(above[:, :128], 63, 0)
+    src6[2] = corner(below[:, 128:], 65, 15)
+    src6[3] = corner(below[:, 128:], 63, 0)
+    pl.semaphore_wait(barrier, N_COL - 1 + N_ROW - 1 + 4)
 
     def remote(src, dst, send, recv, where):
         return pltpu.make_async_remote_copy(
@@ -147,10 +180,17 @@
             device_id_type=MESH,
         )
 
-    south = remote(src1.at[0], dst1.at[0], send1.at[0], recv1.at[0], (row_at(1), col))
-    north = remote(src1.at[1], dst1.at[1], send1.at[1], recv1.at[1], (row_at(N_ROW - 1), col))
-    south.start()
-    north.start()
+    faces = [
+        remote(src6.at[k], dst6.at[k], send6.at[k], recv6.at[k], diagonal[k]) for k in range(4)
+    ]
+    faces += [
+        remote(src2.at[0], dst2.at[0], send2.at[0], recv2.at[0], (row, east_col)),
+        remote(src2.at[1], dst2.at[1], send2.at[1], recv2.at[1], (row, west_col)),
+        remote(src1.at[0], dst1.at[0], send1.at[0], recv1.at[0], (down, col)),
+        remote(src1.at[1], dst1.at[1], send1.at[1], recv1.at[1], (up, col)),
+    ]
+    for copy in faces:
+        copy.start()
 
     arrived(2, 3, 4)
     k_map = dot3(
@@ -163,31 +203,6 @@
         q = q_ref[256 * f : 256 * f + 256, :].astype(F32)
         w = dot3(split(q - tend_ref[256 * f : 256 * f + 256, :]), lift_l)
         own.append(jnp.sum(w * k_map, axis=0, keepdims=True))
-    left, right = nodes_of(0), nodes_of(15)
-
-    south.wait()
-    north.wait()
-    above = jnp.where(lane < 64, jnp.concatenate([dst1[0], dst1[0]], axis=1), above)
-    below = jnp.where(lane >= 192, jnp.concatenate([dst1[1], dst1[1]], axis=1), below)
-    top_new = (top + above) * 0.5
-    bottom_new = (bottom + below) * 0.5
-    left_rows = jnp.where(
-        place == 0, top_new, jnp.where(place == 15, pltpu.roll(bottom_new, 15, 0), left)
-    )
-    right_rows = jnp.where(
-        place == 0, pltpu.roll(top_new, 49, 0), jnp.where(place == 15, bottom_new, right)
-    )
-    to_east = pltpu.roll(right_rows, 193, 1)
-    to_west = pltpu.roll(left_rows, 63, 1)
-    src2[0] = jnp.where(half_lane % 64 == 0, to_east[:, :128], pltpu.roll(to_east[:, 128:], 1, 1))
-    src2[1] = jnp.where(half_lane % 64 == 63, to_west[:, :128], pltpu.roll(to_west[:, 128:], 1, 1))
-    east = remote(src2.at[0], dst2.at[0], send2.at[0], recv2.at[0], (row, (col + 1) % N_COL))
-    west = remote(
-        src2.at[1], dst2.at[1], send2.at[1], recv2.at[1], (row, (col + N_COL - 1) % N_COL)
-    )
-    east.start()
-    west.start()
-
     arrived(6)
     for k in range(LEVELS):
         whole = parent_ref[k]
@@ -196,14 +211,29 @@
         par_h[k] = high
         par_l[k] = low
 
-    east.wait()
-    west.wait()
+    for copy in faces:
+        copy.wait()
+    above = jnp.where(lane < 64, jnp.concatenate([dst1[0], dst1[0]], axis=1), above)
+    below = jnp.where(lane >= 192, jnp.concatenate([dst1[1], dst1[1]], axis=1), below)
+    top_new = (top + above) * 0.5
+    bottom_new = (bottom + below) * 0.5
+    left_rows, right_rows = with_corners(top_new, bottom_new)
 
     def opened(received):
         return jnp.concatenate([received, pltpu.roll(received, 127, 1)], axis=1)
 
+    def spread_corner(k, node, at):
+        rows = dst6[k]
+        rows = jnp.concatenate(
+            [jnp.broadcast_to(rows[f : f + 1], (16, 128)) for f in range(4)], axis=0
+        )
+        here = jnp.logical_and(place == node, lane == at)
+        return jnp.where(here, jnp.concatenate([rows, rows], axis=1) * 0.5, 0.0)
+
     before = jnp.where(lane % 64 == 0, opened(dst2[0]), pltpu.roll(right_rows, 1, 1))
+    before = before + spread_corner(0, 0, 0) + spread_corner(2, 15, 192)
     after = jnp.where(lane % 64 == 63, opened(dst2[1]), pltpu.roll(left_rows, 255, 1))
+    after = after + spread_corner(1, 0, 63) + spread_corner(3, 15, 255)
     inner = jnp.logical_and(place != 0, place != 15)
     deltas = [
         jnp.where(inner, top_new - top, 0.0),
@@ -329,12 +359,14 @@
             pltpu.VMEM((N_COL, 4, 128), F32),
             pltpu.VMEM((4, 128), F32),
             pltpu.VMEM((N_ROW, 4, 128), F32),
+            pltpu.VMEM((4, 4, 128), F32),
+            pltpu.VMEM((4, 4, 128), F32),
             pltpu.VMEM((LEVELS, 256, 128), BF16),
             pltpu.VMEM((LEVELS, 256, 128), BF16),
             pltpu.VMEM((2048, 128), BF16),
             pltpu.VMEM((2048, 128), BF16),
             dma((2,)), dma((2,)), dma((2,)), dma((2,)),
-            dma((N_COL,)), dma((N_COL,)), dma((N_ROW,)), dma((N_ROW,)),
+            dma((N_COL,)), dma((N_COL,)), dma((N_ROW,)), dma((N_ROW,)), dma((4,)), dma((4,)),
         ],
         compiler_params=pltpu.CompilerParams(
             collective_id=0, has_side_effects=True, vmem_limit_bytes=48 * 1024 * 1024

time: 36.8 us -> 34.2 us (0.929)
  Pallas kernels: 35.9 us -> 33.3 us
    pallas_call x1, Pallas kernels: 35.9 us -> 33.3 us  [local(): pl.pallas_call(kernel, name='imex_step', out_shape=jax.ShapeDtypeStruct((...]
where the time goes in v5:
time: 34.2 us; the launch traced here: 34.1 us
  Pallas kernels  33.3 us (97%)
  local copies, waits for them, and re-layouts  0.8 us (2%)
    pallas_call x1, Pallas kernels, local(): pl.pallas_call(kernel, name='imex_step', out_shape=jax.ShapeDtypeStruct((...  33.3 us
    unnamed x1, local copies, waits for them, and re-layouts  0.8 us

profile of v5, /device:TPU:1, one launch (start us, length us, event | category | flops | bytes accessed | tf_op | source)
XLA Modules:
  0.0 34.1 jit_solution(15743301176114743230)
XLA Ops:
  0.0 33.3 %imex_step.1 = bf16[1024,256]{1,0:T(8,128)(2,1)S(1)} custom-call(bf16[1024,256]{1,0:T(8,128)(2,1)} %bitcast.6, f32[256,256]{1,0:T(8,128)} %refs_1_.1, f32[64,256]{1,0:T(8,128)} %refs_2_.1, f32[64,128]{1,0:T(8,128)} %refs_3_.1, f32[256,128]{1,0:T(8,128)} %refs_4_.1, f32[5,128,128]{2,1,0:T(8,128)} %refs_5_.1, f32[5,256,128]{2,1,0:T(8,128)} %refs_6_.1, ...), custom_call_target="tpu_custom_call" | custom-call | tf_op jit(solution)/shard_map/imex_step/pallas_call | solution.py:342
  33.3 0.8 %copy.18 = bf16[4,16,16,1,1,256]{5,2,4,3,1,0:T(8,128)(2,1)} copy(bf16[4,16,16,1,1,256]{5,2,4,3,1,0:T(8,128)(2,1)S(1)} %bitcast.5) | data formatting | bytes 1048576

commit v6 on v5

--- a/solution.py
+++ b/solution.py
@@ -13,6 +13,10 @@
 N_ROW = 16
 N_COL = 32
 advect_scale = 0.01
+Y_STEPS = (0, 1, 2, 3, 4, 3, 2, 3)
+X_STEPS = (0, 1, 2, 1)
+FAR_FIRST = sorted(range(1, N_COL), key=lambda m: -(Y_STEPS[m % 8] + X_STEPS[m // 8]))
+ROWS_FAR_FIRST = sorted(range(1, N_ROW), key=lambda d: -min(d, N_ROW - d))
 
 
 def chebyshev_matrix(node_count):
@@ -104,9 +108,9 @@
         loads[i].start()
 
     barrier = pltpu.get_barrier_semaphore()
-    for m in range(1, N_COL):
+    for m in FAR_FIRST:
         pl.semaphore_signal(barrier, inc=1, device_id=(row, other(m)), device_id_type=MESH)
-    for d in range(1, N_ROW):
+    for d in ROWS_FAR_FIRST:
         pl.semaphore_signal(barrier, inc=1, device_id=(row_at(d), col), device_id_type=MESH)
     down, up = row_at(1), row_at(N_ROW - 1)
     east_col, west_col = (col + 1) % N_COL, (col + N_COL - 1) % N_COL
@@ -254,7 +258,7 @@
     src3[...] = skeleton
     dst3[0] = skeleton
     gathers = []
-    for m in range(N_COL - 1, 0, -1):
+    for m in FAR_FIRST:
         slot = bit_reversed(m)
         gathers.append(
             remote(src3, dst3.at[slot], send3.at[m], recv3.at[m], (row, other(m)))
@@ -305,21 +309,33 @@
     src4[...] = x
     dst4[row] = x
     sends = []
-    arrivals = []
-    for d in range(1, N_ROW):
+    arrivals = {}
+    for d in ROWS_FAR_FIRST:
         sends.append(remote(src4, dst4.at[row], send4.at[d], recv4.at[d], (row_at(d), col)))
-        arrivals.append(
-            remote(src4, dst4.at[row_at(N_ROW - d)], send4.at[d], recv4.at[d], (row_at(d), col))
+        arrivals[d] = remote(
+            src4, dst4.at[row_at(N_ROW - d)], send4.at[d], recv4.at[d], (row_at(d), col)
         )
     for copy in sends:
         copy.start()
     boundary = few_rows_dot3(jnp.concatenate(differences, axis=1), interface_map)
+
+    def solved_from(steps):
+        rows = [row_at(N_ROW - d) for d in steps]
+        spans = [pl.ds(pl.multiple_of(g * 128, 128), 128) for g in rows]
+        operator = [
+            jnp.concatenate([ref[span, :] for span in spans], axis=0) for ref in (top_h, top_l)
+        ]
+        return few_rows_dot3(jnp.concatenate([dst4[g] for g in rows], axis=1), operator)
+
+    far, near = ROWS_FAR_FIRST[:3], ROWS_FAR_FIRST[3:]
     for copy in gathers + sends:
         copy.wait_send()
-    for copy in arrivals:
-        copy.wait_recv()
-    pieces = jnp.concatenate([dst4[g] for g in range(N_ROW)], axis=1)
-    boundary = boundary + few_rows_dot3(pieces, (top_h[...], top_l[...]))
+    for d in near:
+        arrivals[d].wait_recv()
+    boundary = boundary + solved_from([N_ROW] + near)
+    for d in far:
+        arrivals[d].wait_recv()
+    boundary = boundary + solved_from(far)
     for f in range(4):
         weighted = split(extend * boundary[f : f + 1, :])
         at = slice(256 * f, 256 * f + 256)

time: 34.2 us -> 33.9 us (level)
  no operation moved by 1% of the time
where the time goes in v6:
time: 33.9 us; the launch traced here: 33.8 us
  Pallas kernels  33 us (97%)
  local copies, waits for them, and re-layouts  0.8 us (2%)
    pallas_call x1, Pallas kernels, local(): pl.pallas_call(kernel, name='imex_step', out_shape=jax.ShapeDtypeStruct((...  33 us
    unnamed x1, local copies, waits for them, and re-layouts  0.8 us

profile of v6, /device:TPU:1, one launch (start us, length us, event | category | flops | bytes accessed | tf_op | source)
XLA Modules:
  0.0 33.8 jit_solution(11703889666124419564)
XLA Ops:
  0.0 33.0 %imex_step.1 = bf16[1024,256]{1,0:T(8,128)(2,1)S(1)} custom-call(bf16[1024,256]{1,0:T(8,128)(2,1)} %bitcast.6, f32[256,256]{1,0:T(8,128)} %refs_1_.1, f32[64,256]{1,0:T(8,128)} %refs_2_.1, f32[64,128]{1,0:T(8,128)} %refs_3_.1, f32[256,128]{1,0:T(8,128)} %refs_4_.1, f32[5,128,128]{2,1,0:T(8,128)} %refs_5_.1, f32[5,256,128]{2,1,0:T(8,128)} %refs_6_.1, ...), custom_call_target="tpu_custom_call" | custom-call | tf_op jit(solution)/shard_map/imex_step/pallas_call | solution.py:358
  33.0 0.8 %copy.18 = bf16[4,16,16,1,1,256]{5,2,4,3,1,0:T(8,128)(2,1)} copy(bf16[4,16,16,1,1,256]{5,2,4,3,1,0:T(8,128)(2,1)S(1)} %bitcast.5) | data formatting | bytes 1048576

commit v7 on v6

--- a/solution.py
+++ b/solution.py
@@ -146,8 +146,8 @@
     top, bottom = rows_of(0), rows_of(240)
     above = pltpu.roll(bottom, 64, 1)
     below = pltpu.roll(top, 192, 1)
-    src1[0] = above[:, :128]
-    src1[1] = below[:, 128:]
+    src1[0] = above[:, :128].astype(BF16)
+    src1[1] = below[:, 128:].astype(BF16)
 
     left, right = nodes_of(0), nodes_of(15)
 
@@ -166,8 +166,12 @@
     )
     to_east = pltpu.roll(right_part, 193, 1)
     to_west = pltpu.roll(left_part, 63, 1)
-    src2[0] = jnp.where(half_lane % 64 == 0, to_east[:, :128], pltpu.roll(to_east[:, 128:], 1, 1))
-    src2[1] = jnp.where(half_lane % 64 == 63, to_west[:, :128], pltpu.roll(to_west[:, 128:], 1, 1))
+    src2[0] = jnp.where(
+        half_lane % 64 == 0, to_east[:, :128], pltpu.roll(to_east[:, 128:], 1, 1)
+    ).astype(BF16)
+    src2[1] = jnp.where(
+        half_lane % 64 == 63, to_west[:, :128], pltpu.roll(to_west[:, 128:], 1, 1)
+    ).astype(BF16)
 
     def corner(rows, shift, node):
         return pltpu.roll(rows, shift, 1).reshape(4, 16, 128)[:, node, :]
@@ -217,8 +221,8 @@
 
     for copy in faces:
         copy.wait()
-    above = jnp.where(lane < 64, jnp.concatenate([dst1[0], dst1[0]], axis=1), above)
-    below = jnp.where(lane >= 192, jnp.concatenate([dst1[1], dst1[1]], axis=1), below)
+    above = jnp.where(lane < 64, jnp.concatenate([dst1[0], dst1[0]], axis=1).astype(F32), above)
+    below = jnp.where(lane >= 192, jnp.concatenate([dst1[1], dst1[1]], axis=1).astype(F32), below)
     top_new = (top + above) * 0.5
     bottom_new = (bottom + below) * 0.5
     left_rows, right_rows = with_corners(top_new, bottom_new)
@@ -234,9 +238,9 @@
         here = jnp.logical_and(place == node, lane == at)
         return jnp.where(here, jnp.concatenate([rows, rows], axis=1) * 0.5, 0.0)
 
-    before = jnp.where(lane % 64 == 0, opened(dst2[0]), pltpu.roll(right_rows, 1, 1))
+    before = jnp.where(lane % 64 == 0, opened(dst2[0].astype(F32)), pltpu.roll(right_rows, 1, 1))
     before = before + spread_corner(0, 0, 0) + spread_corner(2, 15, 192)
-    after = jnp.where(lane % 64 == 63, opened(dst2[1]), pltpu.roll(left_rows, 255, 1))
+    after = jnp.where(lane % 64 == 63, opened(dst2[1].astype(F32)), pltpu.roll(left_rows, 255, 1))
     after = after + spread_corner(1, 0, 63) + spread_corner(3, 15, 255)
     inner = jnp.logical_and(place != 0, place != 15)
     deltas = [
@@ -367,10 +371,10 @@
             pltpu.VMEM((1024, 256), F32),
             pltpu.VMEM((1024, 256), F32),
             pltpu.VMEM((256, 128), F32),
-            pltpu.VMEM((2, 64, 128), F32),
-            pltpu.VMEM((2, 64, 128), F32),
-            pltpu.VMEM((2, 64, 128), F32),
-            pltpu.VMEM((2, 64, 128), F32),
+            pltpu.VMEM((2, 64, 128), BF16),
+            pltpu.VMEM((2, 64, 128), BF16),
+            pltpu.VMEM((2, 64, 128), BF16),
+            pltpu.VMEM((2, 64, 128), BF16),
             pltpu.VMEM((4, 128), F32),
             pltpu.VMEM((N_COL, 4, 128), F32),
             pltpu.VMEM((4, 128), F32),

time: 33.9 us -> 33.8 us (level)
  no operation moved by 1% of the time
where the time goes in v7:
time: 33.8 us; the launch traced here: 33.7 us
  Pallas kernels  32.9 us (97%)
  local copies, waits for them, and re-layouts  0.8 us (2%)
    pallas_call x1, Pallas kernels, local(): pl.pallas_call(kernel, name='imex_step', out_shape=jax.ShapeDtypeStruct((...  32.9 us
    unnamed x1, local copies, waits for them, and re-layouts  0.8 us

profile of v7, /device:TPU:1, one launch (start us, length us, event | category | flops | bytes accessed | tf_op | source)
XLA Modules:
  0.0 33.7 jit_solution(1095490389297941988)
XLA Ops:
  0.0 32.9 %imex_step.1 = bf16[1024,256]{1,0:T(8,128)(2,1)S(1)} custom-call(bf16[1024,256]{1,0:T(8,128)(2,1)} %bitcast.6, f32[256,256]{1,0:T(8,128)} %refs_1_.1, f32[64,256]{1,0:T(8,128)} %refs_2_.1, f32[64,128]{1,0:T(8,128)} %refs_3_.1, f32[256,128]{1,0:T(8,128)} %refs_4_.1, f32[5,128,128]{2,1,0:T(8,128)} %refs_5_.1, f32[5,256,128]{2,1,0:T(8,128)} %refs_6_.1, ...), custom_call_target="tpu_custom_call" | custom-call | tf_op jit(solution)/shard_map/imex_step/pallas_call | solution.py:362
  32.9 0.8 %copy.18 = bf16[4,16,16,1,1,256]{5,2,4,3,1,0:T(8,128)(2,1)} copy(bf16[4,16,16,1,1,256]{5,2,4,3,1,0:T(8,128)(2,1)S(1)} %bitcast.5) | data formatting | bytes 1048576
